TPU v7x, 32 devices: a whole 2x2x4 slice. The times are simulated.
32 devices in a mesh: sy: 8 (over z, y), sx: 4 (over x, core).
Axes of the slice: x: 2, y: 2, z: 4, core: 2. Of those that a mesh axis runs over, the one named last changes fastest.
Arguments:
- object_re: float32 [2048, 1024], P('sy', 'sx'), may hold values from -6 to 6
- object_im: float32 [2048, 1024], P('sy', 'sx'), may hold values from -6 to 6
- probe_re: float32 [2, 256, 256], replicated, may hold values from -6 to 6
- probe_im: float32 [2, 256, 256], replicated, may hold values from -6 to 6
- amplitudes: float32 [8, 4, 8, 256, 256], P('sy', 'sx'), may hold values from 0.5 to 3
- offsets: int32 [8, 4, 8, 2], P('sy', 'sx'), may hold values from -128 to 127
- visit_order: int32 [8, 4, 8], P('sy', 'sx'), may hold values from 0 to 7, each once within a row
Outputs:
- object_new_re: float32 [2048, 1024], P('sy', 'sx')
- object_new_im: float32 [2048, 1024], P('sy', 'sx')
- probe_new_re: float32 [2, 256, 256], replicated
- probe_new_im: float32 [2, 256, 256], replicated
Inputs may be any that keep to these rules, and one draw needn't show every extreme that they name: `visit_order`: each tile's entries are a permutation of 0 to 7.
All inputs are finite; a program needn't handle non-finite values.
Results may differ from a plain program's by a relative error of at most 0.0019.
Values sent between devices are 32-bit elements; how exact they have to be, the bound alone decides.
No kernel may reach another device: no remote copies, remote signals or barrier semaphores. Data moves between devices by JAX's collectives and lax.ppermute only.
A program may use at most 64 MiB of HBM per device.

v0:
```python
import functools
import math

import jax
import jax.numpy as jnp
from jax import lax
from jax.experimental import pallas as pl
from jax.experimental.pallas import tpu as pltpu
from jax.sharding import PartitionSpec as P

BATCHES = 2
SY, SX = "sy", "sx"

OBJECT_RATE = 0.25
PROBE_GAIN = 4.0

VMEM = pl.BlockSpec(memory_space=pltpu.VMEM)
SMEM = pl.BlockSpec(memory_space=pltpu.SMEM)
HBM = pl.BlockSpec(memory_space=pltpu.HBM)


def call(kernel, out_shape, operands, in_specs=None, scratch=(), room=0):
    outs = jax.tree.leaves(out_shape)
    specs = in_specs or [VMEM] * len(operands)
    held = [a for a, spec in zip(operands, specs) if spec is VMEM]
    need = sum(a.dtype.itemsize * math.prod(a.shape) for a in held + outs) + room
    return pl.pallas_call(
        kernel,
        out_shape=out_shape,
        in_specs=specs,
        out_specs=jax.tree.map(lambda _: VMEM, out_shape),
        scratch_shapes=scratch,
        compiler_params=pltpu.CompilerParams(vmem_limit_bytes=need + (1 << 20)),
    )(*operands)


def f32(*shape):
    return jax.ShapeDtypeStruct(shape, jnp.float32)


def prepare_kernel(
    order, order_hbm, offs_hbm, re_hbm, im_hbm, amp_hbm,
    table_left, table_right, scale, order_out, offs, probe_re, probe_im, amp, sems,
):
    f = probe_re.shape[1]
    moves = [(order_hbm, order_out), (offs_hbm, offs), (re_hbm, probe_re), (im_hbm, probe_im)]
    moves += [(amp_hbm.at[0, 0, order[0, 0, j]], amp.at[j]) for j in range(amp.shape[0])]
    copies = [pltpu.make_async_copy(a, b, sems.at[i]) for i, (a, b) in enumerate(moves)]
    for copy in copies:
        copy.start()
    rows = lax.broadcasted_iota(jnp.int32, (f, f), 0)
    cols = lax.broadcasted_iota(jnp.int32, (f, f), 1)
    phase_angle = 2.0 * math.pi / f * lax.rem(rows * cols, f).astype(jnp.float32)
    norm_scale = 1.0 / math.sqrt(f)
    table_re = (jnp.cos(phase_angle) * norm_scale).astype(jnp.bfloat16)
    table_im = (-jnp.sin(phase_angle) * norm_scale).astype(jnp.bfloat16)
    for table, sign in ((table_left, 1), (table_right, -1)):
        table[:f, :f] = table_re
        table[f:, f:] = table_re
        table[:f, f:] = table_im if sign < 0 else -table_im
        table[f:, :f] = table_im if sign > 0 else -table_im
    for copy in copies:
        copy.wait()
    power = sum(part[m] * part[m] for part in (probe_re, probe_im) for m in range(2))
    scale[...] = OBJECT_RATE / jnp.broadcast_to(jnp.max(power), scale.shape)


def pair_exchange(block, axis, odd, bit=2):
    count_y, count_x = lax.axis_size(SY), lax.axis_size(SX)
    perm = []
    for y in range(count_y):
        for x in range(count_x):
            index, count = (y, count_y) if axis == SY else (x, count_x)
            partner = index + 1 if index % 2 == odd else index - 1
            if 0 <= partner < count:
                to_y, to_x = (partner, x) if axis == SY else (y, partner)
            else:
                to_y, to_x = (y, stand_in(x, count_x, bit)) if axis == SY else (stand_in(y, count_y, bit), x)
            perm.append((y * count_x + x, to_y * count_x + to_x))
    return lax.ppermute(block, (SY, SX), perm)


def stand_in(index, count, bit):
    other = index ^ bit
    return other if other < count else index


def has_partner(axis, odd):
    index, count = lax.axis_index(axis), lax.axis_size(axis)
    partner = jnp.where(lax.rem(index, 2) == odd, index + 1, index - 1)
    return (partner >= 0) & (partner < count)


def masked(axis, odd, block):
    return jnp.where(has_partner(axis, odd), block, 0.0)


def parity(axis):
    return lax.rem(lax.axis_index(axis), 2)


def aligned(value, unit):
    return pl.multiple_of(value, unit)


def pack_tile_kernel(h, obj_re, obj_im, *outs_and_sems):
    outs, sems = outs_and_sems[:-1], outs_and_sems[-1]
    y_even, y_odd, x_even, x_odd, tile = outs[:2], outs[2:4], outs[4], outs[5], outs[6]
    py, px = parity(SY), parity(SX)
    copies = []
    for c, obj in enumerate((obj_re, obj_im)):
        for out, side in ((y_even[c], 1 - py), (y_odd[c], py)):
            rows = pl.ds(aligned(side * h, h), h)
            copies += [(obj.at[rows, pl.ds(lb * h, h)], out.at[lb]) for lb in range(2)]
        for out, side in ((x_even, 1 - px), (x_odd, px)):
            copies.append((obj.at[:, pl.ds(aligned(side * h, h), h)], out.at[c]))
        copies += [(obj.at[:, pl.ds(lb * h, h)], tile.at[c, lb]) for lb in range(2)]
    copies = [pltpu.make_async_copy(a, b, sems.at[i]) for i, (a, b) in enumerate(copies)]
    for copy in copies:
        copy.start()
    for copy in copies:
        copy.wait()


def pack_corner_kernel(up_even, up_odd, c_even, c_odd):
    px = parity(SX)
    for odd, strip in enumerate((up_even, up_odd)):
        c_even[odd] = masked(SY, odd, strip[1 - px])
        c_odd[odd] = masked(SY, odd, strip[px])


def batch_body(
    batch, size, order, offs, probe, tables, amp, ext, accum, grads, grads_before, scratch
):
    sets = [scratch[i::2] for i in range(2)]
    f = probe[0].shape[1]
    h = f // 2
    rows = 16
    lane = lax.broadcasted_iota(jnp.int32, (rows, h), 1)
    table_left, table_right = tables

    def place(j):
        chosen = order[0, 0, batch * size + j]
        left = offs[0, 0, 1, chosen] + h
        return offs[0, 0, 0, chosen] + h, lax.div(left, h), lax.rem(left, h)

    def exits_of(j):
        patch, exits, *_ = sets[j % 2]
        top, first, shift = place(j)
        back_shift = lax.rem(h - shift, h)
        inside = lane < h - shift
        for r in range(0, f, rows):
            here = pl.ds(r, rows)
            window = []
            for c in range(2):
                a, b, d = [
                    pltpu.roll(ext[c, first + k, pl.ds(top + r, rows), :], back_shift, 1) for k in range(3)
                ]
                window.append([jnp.where(inside, a, b), jnp.where(inside, b, d)])
            for lb in range(2):
                o_re, o_im = window[0][lb], window[1][lb]
                patch[0, here, pl.ds(lb * h, h)] = o_re
                patch[1, here, pl.ds(lb * h, h)] = o_im
                for m in range(2):
                    p_re, p_im = [part[m, here, pl.ds(lb * h, h)] for part in probe]
                    spot = pl.ds(m * f + lb * h, h)
                    exits[pl.ds(r, rows), spot] = (p_re * o_re - p_im * o_im).astype(jnp.bfloat16)
                    exits[pl.ds(f + r, rows), spot] = (p_re * o_im + p_im * o_re).astype(jnp.bfloat16)

    def transform(j, values, first_table, second_table):
        mixed, field = sets[j % 2][3:]
        product = jnp.dot(first_table[...], values[...], preferred_element_type=jnp.float32)
        for c in range(2):
            for m in range(2):
                part = product[c * f : (c + 1) * f, m * f : (m + 1) * f]
                mixed[pl.ds(m * f, f), pl.ds(c * f, f)] = part.astype(jnp.bfloat16)
        field[...] = jnp.dot(mixed[...], second_table[...], preferred_element_type=jnp.float32)

    def forward(j):
        transform(j, sets[j % 2][1], table_left, table_right)

    def backward(j):
        transform(j, sets[j % 2][2], table_right, table_left)

    def correct(j):
        _, _, fixed, _, field = sets[j % 2]
        for r in range(0, f, rows):
            for lb in range(2):
                far = [
                    [field[pl.ds(m * f + r, rows), pl.ds(c * f + lb * h, h)] for c in range(2)] for m in range(2)
                ]
                power = sum(part * part for mode in far for part in mode)
                ratio = amp[j, pl.ds(r, rows), pl.ds(lb * h, h)] * lax.rsqrt(jnp.maximum(power, 1.0))
                for m in range(2):
                    for c in range(2):
                        spot = pl.ds(m * f + lb * h, h)
                        fixed[pl.ds(c * f + r, rows), spot] = (far[m][c] * ratio).astype(jnp.bfloat16)

    def gradients(j):
        patch, exits, _, _, field = sets[j % 2]
        top, first, shift = place(j)
        beyond = lane >= shift
        for r in range(0, f, rows):
            here = pl.ds(r, rows)
            term = [[0.0, 0.0], [0.0, 0.0]]
            for lb in range(2):
                cols = pl.ds(lb * h, h)
                o_re, o_im = patch[0, here, cols], patch[1, here, cols]
                for m in range(2):
                    d_re, d_im = [
                        field[pl.ds(m * f + r, rows), pl.ds(c * f + lb * h, h)]
                        - exits[pl.ds(c * f + r, rows), pl.ds(m * f + lb * h, h)].astype(jnp.float32)
                        for c in range(2)
                    ]
                    p_re, p_im = [part[m, here, cols] for part in probe]
                    term[0][lb] += p_re * d_re + p_im * d_im
                    term[1][lb] += p_re * d_im - p_im * d_re
                    for c, part in enumerate((o_re * d_re + o_im * d_im, o_re * d_im - o_im * d_re)):
                        sofar = grads if j else grads_before
                        grads[m, c, lb, here, :] = part if sofar is None else sofar[m, c, lb, here, :] + part
            for c in range(2):
                a, b = [pltpu.roll(part, shift, 1) for part in term[c]]
                there = pl.ds(top + r, rows)
                accum[c, first, there, :] += jnp.where(beyond, a, 0.0)
                accum[c, first + 1, there, :] += jnp.where(beyond, b, a)
                accum[c, first + 2, there, :] += jnp.where(beyond, 0.0, b)

    exits_of(0)
    for j in range(0, size, 2):
        pair = j + 1 < size
        forward(j)
        if j == 0:
            accum[...] = jnp.zeros_like(accum)
        else:
            gradients(j - 1)
        if pair:
            exits_of(j + 1)
            forward(j + 1)
        correct(j)
        backward(j)
        if pair:
            correct(j + 1)
            backward(j + 1)
        gradients(j)
        if j + 2 < size:
            exits_of(j + 2)
        elif pair:
            gradients(j + 1)


def first_batch_kernel(
    h, size, order, offs, tile, up_even_re, up_even_im, up_odd_re, up_odd_im, x_even, x_odd,
    c_even_re, c_even_im, c_odd_re, c_odd_im, probe_re, probe_im, table_left, table_right, amp, amp_hbm,
    ext, accum, send_even, send_00, send_01, send_10, send_11, grads, amp_next, amp_sems, *scratch,
):
    py, px = parity(SY), parity(SX)
    copies = [
        pltpu.make_async_copy(amp_hbm.at[0, 0, order[0, 0, size + j]], amp_next.at[j], amp_sems.at[j]) for j in range(size)
    ]
    for copy in copies:
        copy.start()
    halo_rows = [pl.ds(aligned(side * 3 * h, h), h) for side in (1 - py, py)]
    ups = ((up_even_re, up_odd_re), (up_even_im, up_odd_im))
    corners = ((c_even_re, c_odd_re), (c_even_im, c_odd_im))
    for c in range(2):
        for lb in range(2):
            ext[c, 1 + lb, h : 3 * h] = tile[c, lb]
            for odd in range(2):
                ext[c, 1 + lb, halo_rows[odd]] = masked(SY, odd, ups[c][odd][lb])
        for odd, (block, column) in enumerate((((1 - px) * 3, x_even), (px * 3, x_odd))):
            ext[c, block, h : 3 * h] = masked(SX, odd, column[c])
            for odd_row in range(2):
                ext[c, block, halo_rows[odd_row]] = masked(SX, odd, corners[c][odd][odd_row])
    probe, tables = (probe_re, probe_im), (table_left, table_right)
    batch_body(0, size, order, offs, probe, tables, amp, ext, accum, grads, None, scratch)
    for copy in copies:
        copy.wait()
    for c, sends in enumerate(((send_00, send_01), (send_10, send_11))):
        send_even[c] = accum[c, (1 - px) * 3]
        for odd, send in enumerate(sends):
            send[...] = accum[c, px * 3, half_rows(h, odd)]


def last_batch_kernel(
    h, size, batch, order, offs, columns_00, columns_01, columns_10, columns_11, x_even, odd_00, odd_01, odd_10, odd_11,
    grads_in, probe_re, probe_im, table_left, table_right, amp, accum, send_even, send_odd, keep, give, ext, grads, *scratch,
):
    px = parity(SX)
    columns = ((columns_00, columns_01), (columns_10, columns_11))
    x_odd = ((odd_00, odd_01), (odd_10, odd_11))
    for c in range(2):
        for odd in range(2):
            rows = half_rows(h, odd)
            for lb in range(2):
                ext[c, 1 + lb, rows] = columns[c][odd][lb]
            ext[c, (1 - px) * 3, rows] = masked(SX, 0, x_even[c, odd])
            ext[c, px * 3, rows] = masked(SX, 1, x_odd[c][odd][...])
    probe, tables = (probe_re, probe_im), (table_left, table_right)
    batch_body(batch, size, order, offs, probe, tables, amp, ext, accum, grads, grads_in, scratch)
    keep[...] = grads[px]
    give[...] = grads[1 - px]
    for c in range(2):
        send_even[c] = accum[c, (1 - px) * 3]
        send_odd[c] = accum[c, px * 3]


def batch_scratch(f):
    flat = [pltpu.VMEM((2 * f, 2 * f), dtype) for dtype in (jnp.bfloat16,) * 3 + (jnp.float32,)]
    each = [pltpu.VMEM((2, f, f), jnp.float32), *flat]
    return [buffer for buffer in each for _ in range(2)]


def half_side(odd):
    py = parity(SY)
    return py if odd else 1 - py


def half_rows(h, odd):
    return pl.ds(aligned(half_side(odd) * 2 * h, 2 * h), 2 * h)


def fold_columns_kernel(h, c, odd, accum, x_even, x_odd, y_send):
    px = parity(SX)
    rows = half_rows(h, odd)
    columns = masked(SX, 0, x_even[c, rows]), masked(SX, 1, x_odd[...])
    for block, column in zip((1 - px, px), columns):
        y_send[block] = accum[c, 1 + block, rows] + column


def update_kernel(h, c, odd, scale, y_send, y_got, ext, columns, x_send):
    px, side = parity(SX), half_side(odd)
    rate = scale[0:1, :]
    rate_halo = jnp.where(has_partner(SY, odd), rate, 0.0)
    for lb in range(2):
        for at, factor in ((1 - side, rate), (side, rate_halo)):
            here = pl.ds(aligned(at * h, h), h)
            there = pl.ds(aligned((2 * side + at) * h, h), h)
            total = y_send[lb, here] + masked(SY, odd, y_got[lb, here])
            columns[lb, here] = ext[c, 1 + lb, there] + factor * total
    x_send[...] = columns[px]


def pack_even_kernel(columns_00, columns_01, columns_10, columns_11, x_even):
    px = parity(SX)
    for c, parts in enumerate(((columns_00, columns_01), (columns_10, columns_11))):
        for odd, part in enumerate(parts):
            x_even[c, odd] = part[1 - px]


def fold_last_kernel(h, accum, x_even, x_odd, inner, y_even, y_odd):
    py, px = parity(SY), parity(SX)
    for c in range(2):
        columns = masked(SX, 0, x_even[c]), masked(SX, 1, x_odd[c])
        for block, column in zip((1 - px, px), columns):
            total = accum[c, 1 + block] + column
            inner[c, block] = total[h : 3 * h]
            y_even[c, block] = jnp.where(py == 0, total[3 * h :], total[:h])
            y_odd[c, block] = jnp.where(py == 0, total[:h], total[3 * h :])


def finish_object_kernel(
    h, scale, inner, y_even, y_odd, columns_00, columns_01, columns_10, columns_11, out_re, out_im
):
    rate = scale[0:1, :]
    columns = ((columns_00, columns_01), (columns_10, columns_11))
    for c, out in enumerate((out_re, out_im)):
        for lb in range(2):
            for odd, got in enumerate((y_even, y_odd)):
                side = half_side(odd)
                here = pl.ds(aligned(side * h, h), h)
                old = columns[c][odd][lb, pl.ds(aligned((1 - side) * h, h), h)]
                total = inner[c, lb, here] + masked(SY, odd, got[c, lb])
                out[here, lb * h : (lb + 1) * h] = old + rate * total


def plan_bits():
    bits = {axis: lax.axis_size(axis).bit_length() - 1 for axis in (SY, SX)}
    for axis, count in bits.items():
        if 1 << count != lax.axis_size(axis):
            raise ValueError("axis size")
    first, *across = [(SX, bit) for bit in range(bits[SX])]
    along = [(SY, bit) for bit in range(bits[SY])]
    block = along[:2] + across[:1]
    return first, block, along[2:] + across[1:]


def flip_exchange(block, axis, bit):
    count_y, count_x = lax.axis_size(SY), lax.axis_size(SX)
    flip_y, flip_x = (1 << bit, 0) if axis == SY else (0, 1 << bit)
    perm = [(y * count_x + x, (y ^ flip_y) * count_x + (x ^ flip_x)) for y in range(count_y) for x in range(count_x)]
    return lax.ppermute(block, (SY, SX), perm)


def block_exchange(pieces, bits):
    count_y, count_x = lax.axis_size(SY), lax.axis_size(SX)
    mask_y, mask_x = [sum(1 << bit for axis, bit in bits if axis == own) for own in (SY, SX)]
    groups = {}
    for y in range(count_y):
        for x in range(count_x):
            groups.setdefault((y & ~mask_y, x & ~mask_x), []).append(y * count_x + x)
    return lax.all_to_all(pieces, (SY, SX), 0, 0, tiled=True, axis_index_groups=list(groups.values()))


def sum_kernel(left, right, out):
    out[...] = left[...] + right[...]


def sum_block_kernel(pieces, out):
    size = out.shape[0]
    out[...] = sum(pieces[at : at + size, :] for at in range(0, pieces.shape[0], size))


def spread_kernel(left, right, out):
    total = left[...] + right[...]
    size = total.shape[0]
    for at in range(0, out.shape[0], size):
        out[at : at + size, :] = total


def finish_probe_kernel(rate, keep, got, probe_re, probe_im, out_re, out_im):
    px = parity(SX)
    f = probe_re.shape[1]
    h = f // 2
    for mode, part in ((px, keep), (1 - px, got)):
        for c, (probe, out) in enumerate(((probe_re, out_re), (probe_im, out_im))):
            for lb in range(2):
                cols = slice(lb * h, (lb + 1) * h)
                out[mode, :, cols] = probe[mode, :, cols] + rate * part[c, lb]


def local(object_re, object_im, probe_re, probe_im, amplitudes, offsets, visit_order):
    f = probe_re.shape[1]
    h = f // 2
    positions = visit_order.shape[-1]
    size = positions // BATCHES
    table_type = jax.ShapeDtypeStruct((2 * f, 2 * f), jnp.bfloat16)
    in_hbm = functools.partial(pltpu.with_memory_space_constraint, memory_space=pltpu.HBM)
    offsets = offsets.transpose(0, 1, 3, 2)
    arrays = (visit_order, offsets, probe_re, probe_im)
    table_left, table_right, scale, *arrays, amp = call(
        prepare_kernel,
        [table_type, table_type, f32(8, h)] + [jax.ShapeDtypeStruct(a.shape, a.dtype) for a in arrays] + [f32(size, f, f)],
        (visit_order, *map(in_hbm, arrays), in_hbm(amplitudes)),
        [SMEM] + [HBM] * 5,
        [pltpu.SemaphoreType.DMA((4 + size,))],
    )
    visit_order, offsets, *probe = arrays
    strip = f32(2, h, h)
    block = f32(2, 2 * h, h)
    up = call(
        functools.partial(pack_tile_kernel, h),
        [strip] * 4 + [block] * 2 + [f32(2, 2, 2 * h, h)],
        (in_hbm(object_re), in_hbm(object_im)),
        [HBM] * 2,
        [pltpu.SemaphoreType.DMA((16,))],
    )
    up_even = [pair_exchange(up[c], SY, 0) for c in range(2)]
    up_odd = [pair_exchange(up[2 + c], SY, 1) for c in range(2)]
    x_even = pair_exchange(up[4], SX, 0)
    x_odd = pair_exchange(up[5], SX, 1)
    corners = [call(pack_corner_kernel, [strip, strip], (up_even[c], up_odd[c])) for c in range(2)]
    c_even = [pair_exchange(corners[c][0], SX, 0) for c in range(2)]
    c_odd = [pair_exchange(corners[c][1], SX, 1) for c in range(2)]

    column, columns_type = f32(2 * h, h), f32(2, 4 * h, h)
    ext_type, grads_type = f32(2, 4, 4 * h, h), f32(2, 2, 2, f, h)
    fixed_args = (*probe, table_left, table_right)
    fixed_specs = [VMEM] * 4
    ext, accum, send_even, *send_odd, grads, amp_next = call(
        functools.partial(first_batch_kernel, h, size),
        [ext_type, ext_type, columns_type] + [column] * 4 + [grads_type, f32(size, f, f)],
        (visit_order, offsets, up[6], *up_even, *up_odd, x_even, x_odd, *c_even, *c_odd, *fixed_args, amp, in_hbm(amplitudes)),
        [SMEM] * 2 + [VMEM] * 12 + fixed_specs + [HBM],
        [pltpu.SemaphoreType.DMA((size,)), *batch_scratch(f)],
        9 << 20,
    )

    streams = [(c, odd) for c in range(2) for odd in range(2)]
    x_even = pair_exchange(send_even, SX, 0)
    columns, x_odd = [], []
    for (c, odd), part in zip(streams, send_odd):
        x_got = pair_exchange(part, SX, 1)
        y_send = call(functools.partial(fold_columns_kernel, h, c, odd), block, (accum, x_even, x_got))
        y_got = pair_exchange(y_send, SY, odd)
        new, x_send = call(functools.partial(update_kernel, h, c, odd), [block, column], (scale, y_send, y_got, ext))
        columns.append(new)
        x_odd.append(pair_exchange(x_send, SX, 1))
    x_send = call(pack_even_kernel, f32(2, 2, 2 * h, h), columns)
    x_even = pair_exchange(x_send, SX, 0)
    modes = f32(2, 2, f, h)
    accum, send_even, send_odd, keep, give = call(
        functools.partial(last_batch_kernel, h, size, 1),
        [ext_type, columns_type, columns_type, modes, modes],
        (visit_order, offsets, *columns, x_even, *x_odd, grads, *fixed_args, amp_next),
        [SMEM] * 2 + [VMEM] * 11 + fixed_specs,
        [pltpu.VMEM(t.shape, t.dtype) for t in (ext_type, grads_type)] + batch_scratch(f),
        12 << 20,
    )

    x_odd = pair_exchange(send_odd, SX, 1, 1)
    x_even = pair_exchange(send_even, SX, 0)
    last = f32(2, 2, h, h)
    inner, y_even, y_odd = call(
        functools.partial(fold_last_kernel, h), [f32(2, 2, 2 * h, h), last, last], (accum, x_even, x_odd)
    )
    y_even = pair_exchange(y_even, SY, 0)
    y_odd = pair_exchange(y_odd, SY, 1)
    out_re, out_im = call(
        functools.partial(finish_object_kernel, h), [f32(2 * h, 2 * h)] * 2, (scale, inner, y_even, y_odd, *columns)
    )

    first, block_bits, pairs = plan_bits()
    keep, give = keep.reshape(-1, h), give.reshape(-1, h)
    both = call(sum_kernel, f32(*keep.shape), (keep, flip_exchange(give, *first)))
    pieces = block_exchange(both, block_bits)
    total = call(sum_block_kernel, f32(keep.shape[0] >> len(block_bits), h), (pieces,))
    for at, (axis, bit) in enumerate(pairs):
        got = flip_exchange(total, axis, bit)
        last_pair = at == len(pairs) - 1
        kernel, shape = (spread_kernel, keep.shape) if last_pair else (sum_kernel, total.shape)
        total = call(kernel, f32(*shape), (total, got))
    total = block_exchange(total, block_bits)
    got = flip_exchange(total, *first)
    probe_rate = PROBE_GAIN / (positions * math.sqrt(lax.axis_size(SY) * lax.axis_size(SX)))
    piece = (2, 2, f, h)
    probe_out = call(
        functools.partial(finish_probe_kernel, probe_rate),
        [f32(2, f, f)] * 2,
        (total.reshape(piece), got.reshape(piece), *probe),
    )
    return (out_re, out_im, probe_out[0], probe_out[1])


def solution(mesh):
    return jax.shard_map(
        local,
        mesh=mesh,
        in_specs=(
            P(SY, SX),
            P(SY, SX),
            P(),
            P(),
            P(SY, SX, None, None, None),
            P(SY, SX, None, None),
            P(SY, SX, None),
        ),
        out_specs=(P(SY, SX), P(SY, SX), P(), P()),
        check_vma=False,
    )
```

profile of v0, /device:TPU:0, one launch (start us, length us, event | category | flops | bytes accessed | tf_op | source)
XLA Modules:
  0.0 136.9 jit_solution(9364320932727819414)
XLA Ops:
  0.6 1.6 %shard_map.103 = (f32[2,128,128]{2,1,0:T(8,128)S(1)}, f32[2,128,128]{2,1,0:T(8,128)S(1)}, f32[2,128,128]{2,1,0:T(8,128)S(1)}, f32[2,128,128]{2,1,0:T(8,128)S(1)}...) custom-call(f32[256,256]{1,0:T(8,128)} %obj_re.1, f32[256,256]{1,0:T(8,128)} %obj_im.1), custom_call_target="tpu_custom_call" | custom-call | tf_op jit(solution)/shard_map/pallas_call | solution.py:27
  2.2 3.1 %collective-permute-start.1 = (f32[2,128,128]{2,1,0:T(8,128)S(1)}, f32[2,128,128]{2,1,0:T(8,128)S(1)}, u32[]{:S(2)}, u32[]{:S(2)}) collective-permute-start(f32[2,128,128]{2,1,0:T(8,128)S(1)} %get-tuple-element.57), channel_id=1, source_target_pairs={{0,4},{1,5},{2,6},{3,7},{4,0},{5,1},{6,2},{7,3},{8,12},{9,13},{10,... | collective-permute-start | bytes 393224 | tf_op jit(solution)/shard_map/ppermute | solution.py:80
  5.3 1.5 %collective-permute-start.3 = (f32[2,128,128]{2,1,0:T(8,128)S(1)}, f32[2,128,128]{2,1,0:T(8,128)S(1)}, u32[]{:S(2)}, u32[]{:S(2)}) collective-permute-start(f32[2,128,128]{2,1,0:T(8,128)S(1)} %get-tuple-element.59), channel_id=1, source_target_pairs={{0,2},{1,3},{2,0},{3,1},{4,8},{5,9},{6,10},{7,11},{8,4},{9,5},{10,... | collective-permute-start | bytes 393224 | tf_op jit(solution)/shard_map/ppermute | solution.py:80
  6.8 1.5 %collective-permute-start = (f32[2,128,128]{2,1,0:T(8,128)S(1)}, f32[2,128,128]{2,1,0:T(8,128)S(1)}, u32[]{:S(2)}, u32[]{:S(2)}) collective-permute-start(f32[2,128,128]{2,1,0:T(8,128)S(1)} %get-tuple-element.56), channel_id=1, source_target_pairs={{0,4},{1,5},{2,6},{3,7},{4,0},{5,1},{6,2},{7,3},{8,12},{9,13},{10,... | collective-permute-start | bytes 393224 | tf_op jit(solution)/shard_map/ppermute | solution.py:80
  8.3 1.5 %collective-permute-start.2 = (f32[2,128,128]{2,1,0:T(8,128)S(1)}, f32[2,128,128]{2,1,0:T(8,128)S(1)}, u32[]{:S(2)}, u32[]{:S(2)}) collective-permute-start(f32[2,128,128]{2,1,0:T(8,128)S(1)} %get-tuple-element.58), channel_id=1, source_target_pairs={{0,2},{1,3},{2,0},{3,1},{4,8},{5,9},{6,10},{7,11},{8,4},{9,5},{10,... | collective-permute-start | bytes 393224 | tf_op jit(solution)/shard_map/ppermute | solution.py:80
  9.8 5.0 %collective-permute-done.1.up_even.up_even_im = f32[2,128,128]{2,1,0:T(8,128)S(1)} collective-permute-done((f32[2,128,128]{2,1,0:T(8,128)S(1)}, f32[2,128,128]{2,1,0:T(8,128)S(1)}, u32[]{:S(2)}, u32[]{:S(2)}) %collective-permute-start.1) | collective-permute-done | bytes 131104 | tf_op jit(solution)/shard_map/ppermute | solution.py:80
  14.9 0.5 collective-permute-start.4
  15.4 2.0 %collective-permute-start.5 = (f32[2,256,128]{2,1,0:T(8,128)S(1)}, f32[2,256,128]{2,1,0:T(8,128)S(1)}, u32[]{:S(2)}, u32[]{:S(2)}) collective-permute-start(f32[2,256,128]{2,1,0:T(8,128)S(1)} %get-tuple-element.61), channel_id=1, source_target_pairs={{0,8},{1,2},{2,1},{3,11},{4,12},{5,6},{6,5},{7,15},{8,0},{9,10},{1... | collective-permute-start | bytes 786440 | tf_op jit(solution)/shard_map/ppermute | solution.py:80
  17.4 1.6 %collective-permute-start.9 = (f32[2,128,128]{2,1,0:T(8,128)S(1)}, f32[2,128,128]{2,1,0:T(8,128)S(1)}, u32[]{:S(2)}, u32[]{:S(2)}) collective-permute-start(f32[2,128,128]{2,1,0:T(8,128)S(1)} %get-tuple-element.65), channel_id=1, source_target_pairs={{0,8},{1,2},{2,1},{3,11},{4,12},{5,6},{6,5},{7,15},{8,0},{9,10},{1... | collective-permute-start | bytes 393224 | tf_op jit(solution)/shard_map/ppermute | solution.py:80
  19.2 1.6 %collective-permute-start.8 = (f32[2,128,128]{2,1,0:T(8,128)S(1)}, f32[2,128,128]{2,1,0:T(8,128)S(1)}, u32[]{:S(2)}, u32[]{:S(2)}) collective-permute-start(f32[2,128,128]{2,1,0:T(8,128)S(1)} %get-tuple-element.64), channel_id=1, source_target_pairs={{0,8},{1,2},{2,1},{3,11},{4,12},{5,6},{6,5},{7,15},{8,0},{9,10},{1... | collective-permute-start | bytes 393224 | tf_op jit(solution)/shard_map/ppermute | solution.py:80
  20.7 2.5 %shard_map.102 = (bf16[512,512]{1,0:T(8,128)(2,1)S(1)}, bf16[512,512]{1,0:T(8,128)(2,1)S(1)}, f32[8,128]{1,0:T(8,128)S(1)}, s32[1,1,8]{2,1,0:T(1,128)S(1)}, s32[...) custom-call(s32[1,1,8]{2,1,0:T(1,128)} %order_hbm.1, ...), custom_call_target="tpu_custom_call" | custom-call | tf_op jit(solution)/shard_map/pallas_call | solution.py:27
  23.3 1.3 collective-permute-done.8.c_odd_re
  24.6 8.2 %shard_map.106 = (f32[2,4,512,128]{3,2,1,0:T(8,128)S(1)}, f32[2,4,512,128]{3,2,1,0:T(8,128)S(1)}, f32[2,512,128]{2,1,0:T(8,128)S(1)}, f32[256,128]{1,0:T(8,128)S...) custom-call(s32[1,1,8]{2,1,0:T(1,128)S(1)} %get-tuple-element.53.ord, ...), custom_call_target="tpu_custom_call" | custom-call | tf_op jit(solution)/shard_map/pallas_call | solution.py:27
  32.9 2.1 %collective-permute-start.11 = (f32[256,128]{1,0:T(8,128)S(1)}, f32[256,128]{1,0:T(8,128)S(1)}, u32[]{:S(2)}, u32[]{:S(2)}) collective-permute-start(f32[256,128]{1,0:T(8,128)S(1)} %get-tuple-element.73), channel_id=1, source_target_pairs={{0,8},{1,2},{2,1},{3,11},{4,12},{5,6},{6,5},{7,15},{8,0},{9,10},{1... | collective-permute-start | bytes 393224 | tf_op jit(solution)/shard_map/ppermute | solution.py:80
  35.1 1.9 %collective-permute-start.15 = (f32[256,128]{1,0:T(8,128)S(1)}, f32[256,128]{1,0:T(8,128)S(1)}, u32[]{:S(2)}, u32[]{:S(2)}) collective-permute-start(f32[256,128]{1,0:T(8,128)S(1)} %get-tuple-element.78), channel_id=1, source_target_pairs={{0,8},{1,2},{2,1},{3,11},{4,12},{5,6},{6,5},{7,15},{8,0},{9,10},{1... | collective-permute-start | bytes 393224 | tf_op jit(solution)/shard_map/ppermute | solution.py:80
  37.2 0.8 collective-permute-done.11.x_odd
  38.1 2.6 %collective-permute-start.12 = (f32[2,256,128]{2,1,0:T(8,128)S(1)}, f32[2,256,128]{2,1,0:T(8,128)S(1)}, u32[]{:S(2)}, u32[]{:S(2)}) collective-permute-start(f32[2,256,128]{2,1,0:T(8,128)S(1)} %shard_map.107.y_send), channel_id=1, source_target_pairs={{0,4},{1,5},{2,6},{3,7},{4,0},{5,1},{6,2},{7,3},{8,12},{9,13},{10,... | collective-permute-start | bytes 786440 | tf_op jit(solution)/shard_map/ppermute | solution.py:80
  40.7 0.3 collective-permute-start.14
  40.9 0.5 collective-permute-done.15.x_odd
  41.5 2.4 %collective-permute-start.16 = (f32[2,256,128]{2,1,0:T(8,128)S(1)}, f32[2,256,128]{2,1,0:T(8,128)S(1)}, u32[]{:S(2)}, u32[]{:S(2)}) collective-permute-start(f32[2,256,128]{2,1,0:T(8,128)S(1)} %shard_map.111.y_send), channel_id=1, source_target_pairs={{0,4},{1,5},{2,6},{3,7},{4,0},{5,1},{6,2},{7,3},{8,12},{9,13},{10,... | collective-permute-start | bytes 786440 | tf_op jit(solution)/shard_map/ppermute | solution.py:80
  43.9 0.4 collective-permute-start.18
  44.3 14.2 %collective-permute-done.12.y_got = f32[2,256,128]{2,1,0:T(8,128)S(1)} collective-permute-done((f32[2,256,128]{2,1,0:T(8,128)S(1)}, f32[2,256,128]{2,1,0:T(8,128)S(1)}, u32[]{:S(2)}, u32[]{:S(2)}) %collective-permute-start.12) | collective-permute-done | bytes 262176 | tf_op jit(solution)/shard_map/ppermute | solution.py:80
  58.6 0.1 shard_map.110
  58.7 4.6 %collective-permute-done.16.y_got = f32[2,256,128]{2,1,0:T(8,128)S(1)} collective-permute-done((f32[2,256,128]{2,1,0:T(8,128)S(1)}, f32[2,256,128]{2,1,0:T(8,128)S(1)}, u32[]{:S(2)}, u32[]{:S(2)}) %collective-permute-start.16) | collective-permute-done | bytes 262176 | tf_op jit(solution)/shard_map/ppermute | solution.py:80
  63.4 0.1 shard_map.114
  63.6 2.4 %collective-permute-start.20 = (f32[256,128]{1,0:T(8,128)S(1)}, f32[256,128]{1,0:T(8,128)S(1)}, u32[]{:S(2)}, u32[]{:S(2)}) collective-permute-start(f32[256,128]{1,0:T(8,128)S(1)} %get-tuple-element.82), channel_id=1, source_target_pairs={{0,8},{1,2},{2,1},{3,11},{4,12},{5,6},{6,5},{7,15},{8,0},{9,10},{1... | collective-permute-start | bytes 393224 | tf_op jit(solution)/shard_map/ppermute | solution.py:80
  66.1 1.9 %collective-permute-start.22 = (f32[256,128]{1,0:T(8,128)S(1)}, f32[256,128]{1,0:T(8,128)S(1)}, u32[]{:S(2)}, u32[]{:S(2)}) collective-permute-start(f32[256,128]{1,0:T(8,128)S(1)} %get-tuple-element.84), channel_id=1, source_target_pairs={{0,8},{1,2},{2,1},{3,11},{4,12},{5,6},{6,5},{7,15},{8,0},{9,10},{1... | collective-permute-start | bytes 393224 | tf_op jit(solution)/shard_map/ppermute | solution.py:80
  68.1 0.8 collective-permute-done.20.odd_00
  69.0 2.0 %collective-permute-done.21.odd_01 = f32[256,128]{1,0:T(8,128)S(1)} collective-permute-done((f32[256,128]{1,0:T(8,128)S(1)}, f32[256,128]{1,0:T(8,128)S(1)}, u32[]{:S(2)}, u32[]{:S(2)}) %collective-permute-start.21) | collective-permute-done | bytes 131104 | tf_op jit(solution)/shard_map/ppermute | solution.py:80
  71.0 1.4 %collective-permute-done.22.odd_10 = f32[256,128]{1,0:T(8,128)S(1)} collective-permute-done((f32[256,128]{1,0:T(8,128)S(1)}, f32[256,128]{1,0:T(8,128)S(1)}, u32[]{:S(2)}, u32[]{:S(2)}) %collective-permute-start.22) | collective-permute-done | bytes 131104 | tf_op jit(solution)/shard_map/ppermute | solution.py:80
  72.4 1.4 %collective-permute-done.23.odd_11 = f32[256,128]{1,0:T(8,128)S(1)} collective-permute-done((f32[256,128]{1,0:T(8,128)S(1)}, f32[256,128]{1,0:T(8,128)S(1)}, u32[]{:S(2)}, u32[]{:S(2)}) %collective-permute-start.23) | collective-permute-done | bytes 131104 | tf_op jit(solution)/shard_map/ppermute | solution.py:80
  73.8 7.4 %shard_map.116 = (f32[2,4,512,128]{3,2,1,0:T(8,128)S(1)}, f32[2,512,128]{2,1,0:T(8,128)S(1)}, f32[2,512,128]{2,1,0:T(8,128)S(1)}, f32[2,2,256,128]{3,2,1,0:T(8,128)S(1)}, f32[2,2,256,128]{3,2,1,0:T(8,128)S(1)}) custom-call(s32[1,1,8]{2,1,0:T(1,128)S(1)} %get-tuple-element.53.order, s32[1,1,2,8]{3,2,1,0:T(2,128)S(1)} %get-tuple-element.54.offs, ...), custom_call_target="tpu_custom_call" | custom-call | tf_op jit(solution)/shard_map/pallas_call | solution.py:27
  81.3 1.9 %collective-permute-done.28.right = f32[1024,128]{1,0:T(8,128)S(1)} collective-permute-done((f32[1024,128]{1,0:T(8,128)S(1)}, f32[1024,128]{1,0:T(8,128)S(1)}, u32[]{:S(2)}, u32[]{:S(2)}) %collective-permute-start.28) | collective-permute-done | bytes 524320 | tf_op jit(solution)/shard_map/ppermute | solution.py:391
  83.3 13.4 %all_to_all.23 = f32[8,128,128]{2,1,0:T(8,128)S(1)} all-to-all(f32[8,128,128]{2,1,0:T(8,128)S(1)} %bitcast.9), channel_id=1, replica_groups={{0,2,4,6,8,10,12,14},{1,3,5,7,9,11,13,15},{16,18,20,22,24,26,28,30},{17..., dimensions={0} | all-to-all | bytes 1048576 | tf_op jit(solution)/shard_map/all_to_all | solution.py:401
  96.8 1.9 %collective-permute-start.29 = (f32[128,128]{1,0:T(8,128)S(1)}, f32[128,128]{1,0:T(8,128)S(1)}, u32[]{:S(2)}, u32[]{:S(2)}) collective-permute-start(f32[128,128]{1,0:T(8,128)S(1)} %shard_map.120.left), channel_id=1, source_target_pairs={{0,16},{1,17},{2,18},{3,19},{4,20},{5,21},{6,22},{7,23},{8,24},{9,... | collective-permute-start | bytes 196616 | tf_op jit(solution)/shard_map/ppermute | solution.py:391
  98.7 4.0 %collective-permute-done.29.right = f32[128,128]{1,0:T(8,128)S(1)} collective-permute-done((f32[128,128]{1,0:T(8,128)S(1)}, f32[128,128]{1,0:T(8,128)S(1)}, u32[]{:S(2)}, u32[]{:S(2)}) %collective-permute-start.29) | collective-permute-done | bytes 65568 | tf_op jit(solution)/shard_map/ppermute | solution.py:391
  102.7 0.8 shard_map.121
  103.5 3.5 %all-to-all-start.1 = ((f32[8,128,128]{2,1,0:T(8,128)}), f32[8,128,128]{2,1,0:T(8,128)S(1)}, u32[]{:S(2)}, u32[]{:S(2)}) async-start(f32[8,128,128]{2,1,0:T(8,128)} %bitcast.5), calls=%async_computation.1 | async-start | bytes 1048576 | tf_op jit(solution)/shard_map/all_to_all | solution.py:401
  107.1 1.9 %collective-permute-start.25 = (f32[2,512,128]{2,1,0:T(8,128)}, f32[2,512,128]{2,1,0:T(8,128)}, u32[]{:S(2)}, u32[]{:S(2)}) collective-permute-start(f32[2,512,128]{2,1,0:T(8,128)} %copy-done.2), channel_id=1, source_target_pairs={{0,4},{1,2},{2,1},{3,7},{4,0},{5,6},{6,5},{7,3},{8,12},{9,10},{10,... | collective-permute-start | bytes 1572872 | tf_op jit(solution)/shard_map/ppermute | solution.py:80
  109.0 5.8 %all-to-all-done.1 = f32[8,128,128]{2,1,0:T(8,128)S(1)} async-done(((f32[8,128,128]{2,1,0:T(8,128)}), f32[8,128,128]{2,1,0:T(8,128)S(1)}, u32[]{:S(2)}, u32[]{:S(2)}) %all-to-all-start.1) | async-done | bytes 524320 | tf_op jit(solution)/shard_map/all_to_all | solution.py:401
  114.8 4.5 %collective-permute-done.25.x_odd = f32[2,512,128]{2,1,0:T(8,128)} collective-permute-done((f32[2,512,128]{2,1,0:T(8,128)}, f32[2,512,128]{2,1,0:T(8,128)}, u32[]{:S(2)}, u32[]{:S(2)}) %collective-permute-start.25) | collective-permute-done | bytes 524320 | tf_op jit(solution)/shard_map/ppermute | solution.py:80
  119.2 1.6 %copy-done.1 = f32[2,4,512,128]{3,2,1,0:T(8,128)S(1)} copy-done((f32[2,4,512,128]{3,2,1,0:T(8,128)S(1)}, f32[2,4,512,128]{3,2,1,0:T(8,128)}, u32[]{:S(2)}) %copy-start.1) | copy-done | bytes 2097176
  120.8 1.2 shard_map.117
  122.0 1.4 %collective-permute-start.26 = (f32[2,2,128,128]{3,2,1,0:T(8,128)S(1)}, f32[2,2,128,128]{3,2,1,0:T(8,128)S(1)}, u32[]{:S(2)}, u32[]{:S(2)}) collective-permute-start(f32[2,2,128,128]{3,2,1,0:T(8,128)S(1)} %get-tuple-element.92), channel_id=1, source_target_pairs={{0,4},{1,5},{2,6},{3,7},{4,0},{5,1},{6,2},{7,3},{8,12},{9,13},{10,... | collective-permute-start | bytes 786440 | tf_op jit(solution)/shard_map/ppermute | solution.py:80
  123.4 0.7 collective-permute-start.27
  124.1 10.8 %collective-permute-done.26.y_even = f32[2,2,128,128]{3,2,1,0:T(8,128)S(1)} collective-permute-done((f32[2,2,128,128]{3,2,1,0:T(8,128)S(1)}, f32[2,2,128,128]{3,2,1,0:T(8,128)S(1)}, u32[]{:S(2)}, u32[]{:S(2)}) %collective-permute-start.26) | collective-permute-done | bytes 262176 | tf_op jit(solution)/shard_map/ppermute | solution.py:80
  134.9 0.9 shard_map.118
  135.8 1.1 shard_map.122
  (46 shorter events, 1.3 us)
Async XLA Ops:
  2.2 12.5 %collective-permute-start.1 = (f32[2,128,128]{2,1,0:T(8,128)S(1)}, f32[2,128,128]{2,1,0:T(8,128)S(1)}, u32[]{:S(2)}, u32[]{:S(2)}) collective-permute-start(f32[2,128,128]{2,1,0:T(8,128)S(1)} %get-tuple-element.57), channel_id=1, source_target_pairs={{0,4},{1,5},{2,6},{3,7},{4,0},{5,1},{6,2},{7,3},{8,12},{9,13},{10,... | collective-permute-start | bytes 393224 | tf_op jit(solution)/shard_map/ppermute | solution.py:80
  5.3 9.5 %collective-permute-start.3 = (f32[2,128,128]{2,1,0:T(8,128)S(1)}, f32[2,128,128]{2,1,0:T(8,128)S(1)}, u32[]{:S(2)}, u32[]{:S(2)}) collective-permute-start(f32[2,128,128]{2,1,0:T(8,128)S(1)} %get-tuple-element.59), channel_id=1, source_target_pairs={{0,2},{1,3},{2,0},{3,1},{4,8},{5,9},{6,10},{7,11},{8,4},{9,5},{10,... | collective-permute-start | bytes 393224 | tf_op jit(solution)/shard_map/ppermute | solution.py:80
  6.8 10.6 %collective-permute-start = (f32[2,128,128]{2,1,0:T(8,128)S(1)}, f32[2,128,128]{2,1,0:T(8,128)S(1)}, u32[]{:S(2)}, u32[]{:S(2)}) collective-permute-start(f32[2,128,128]{2,1,0:T(8,128)S(1)} %get-tuple-element.56), channel_id=1, source_target_pairs={{0,4},{1,5},{2,6},{3,7},{4,0},{5,1},{6,2},{7,3},{8,12},{9,13},{10,... | collective-permute-start | bytes 393224 | tf_op jit(solution)/shard_map/ppermute | solution.py:80
  8.3 10.7 %collective-permute-start.2 = (f32[2,128,128]{2,1,0:T(8,128)S(1)}, f32[2,128,128]{2,1,0:T(8,128)S(1)}, u32[]{:S(2)}, u32[]{:S(2)}) collective-permute-start(f32[2,128,128]{2,1,0:T(8,128)S(1)} %get-tuple-element.58), channel_id=1, source_target_pairs={{0,2},{1,3},{2,0},{3,1},{4,8},{5,9},{6,10},{7,11},{8,4},{9,5},{10,... | collective-permute-start | bytes 393224 | tf_op jit(solution)/shard_map/ppermute | solution.py:80
  14.8 4.3 %collective-permute-start.7 = (f32[2,128,128]{2,1,0:T(8,128)S(1)}, f32[2,128,128]{2,1,0:T(8,128)S(1)}, u32[]{:S(2)}, u32[]{:S(2)}) collective-permute-start(f32[2,128,128]{2,1,0:T(8,128)S(1)} %get-tuple-element.63), channel_id=1, source_target_pairs={{0,1},{1,0},{2,3},{3,2},{4,5},{5,4},{6,7},{7,6},{8,9},{9,8},{10,11... | collective-permute-start | bytes 393224 | tf_op jit(solution)/shard_map/ppermute | solution.py:80
  14.9 9.7 %collective-permute-start.4 = (f32[2,256,128]{2,1,0:T(8,128)S(1)}, f32[2,256,128]{2,1,0:T(8,128)S(1)}, u32[]{:S(2)}, u32[]{:S(2)}) collective-permute-start(f32[2,256,128]{2,1,0:T(8,128)S(1)} %get-tuple-element.60), channel_id=1, source_target_pairs={{0,1},{1,0},{2,3},{3,2},{4,5},{5,4},{6,7},{7,6},{8,9},{9,8},{10,11... | collective-permute-start | bytes 786440 | tf_op jit(solution)/shard_map/ppermute | solution.py:80
  15.4 9.2 %collective-permute-start.5 = (f32[2,256,128]{2,1,0:T(8,128)S(1)}, f32[2,256,128]{2,1,0:T(8,128)S(1)}, u32[]{:S(2)}, u32[]{:S(2)}) collective-permute-start(f32[2,256,128]{2,1,0:T(8,128)S(1)} %get-tuple-element.61), channel_id=1, source_target_pairs={{0,8},{1,2},{2,1},{3,11},{4,12},{5,6},{6,5},{7,15},{8,0},{9,10},{1... | collective-permute-start | bytes 786440 | tf_op jit(solution)/shard_map/ppermute | solution.py:80
  17.4 5.8 %collective-permute-start.9 = (f32[2,128,128]{2,1,0:T(8,128)S(1)}, f32[2,128,128]{2,1,0:T(8,128)S(1)}, u32[]{:S(2)}, u32[]{:S(2)}) collective-permute-start(f32[2,128,128]{2,1,0:T(8,128)S(1)} %get-tuple-element.65), channel_id=1, source_target_pairs={{0,8},{1,2},{2,1},{3,11},{4,12},{5,6},{6,5},{7,15},{8,0},{9,10},{1... | collective-permute-start | bytes 393224 | tf_op jit(solution)/shard_map/ppermute | solution.py:80
  19.1 4.2 %collective-permute-start.6 = (f32[2,128,128]{2,1,0:T(8,128)S(1)}, f32[2,128,128]{2,1,0:T(8,128)S(1)}, u32[]{:S(2)}, u32[]{:S(2)}) collective-permute-start(f32[2,128,128]{2,1,0:T(8,128)S(1)} %get-tuple-element.62), channel_id=1, source_target_pairs={{0,1},{1,0},{2,3},{3,2},{4,5},{5,4},{6,7},{7,6},{8,9},{9,8},{10,11... | collective-permute-start | bytes 393224 | tf_op jit(solution)/shard_map/ppermute | solution.py:80
  19.2 5.4 %collective-permute-start.8 = (f32[2,128,128]{2,1,0:T(8,128)S(1)}, f32[2,128,128]{2,1,0:T(8,128)S(1)}, u32[]{:S(2)}, u32[]{:S(2)}) collective-permute-start(f32[2,128,128]{2,1,0:T(8,128)S(1)} %get-tuple-element.64), channel_id=1, source_target_pairs={{0,8},{1,2},{2,1},{3,11},{4,12},{5,6},{6,5},{7,15},{8,0},{9,10},{1... | collective-permute-start | bytes 393224 | tf_op jit(solution)/shard_map/ppermute | solution.py:80
  32.8 5.2 %collective-permute-start.10 = (f32[2,512,128]{2,1,0:T(8,128)S(1)}, f32[2,512,128]{2,1,0:T(8,128)S(1)}, u32[]{:S(2)}, u32[]{:S(2)}) collective-permute-start(f32[2,512,128]{2,1,0:T(8,128)S(1)} %get-tuple-element.72), channel_id=1, source_target_pairs={{0,1},{1,0},{2,3},{3,2},{4,5},{5,4},{6,7},{7,6},{8,9},{9,8},{10,11... | collective-permute-start | bytes 1572872 | tf_op jit(solution)/shard_map/ppermute | solution.py:80
  32.9 5.1 %collective-permute-start.11 = (f32[256,128]{1,0:T(8,128)S(1)}, f32[256,128]{1,0:T(8,128)S(1)}, u32[]{:S(2)}, u32[]{:S(2)}) collective-permute-start(f32[256,128]{1,0:T(8,128)S(1)} %get-tuple-element.73), channel_id=1, source_target_pairs={{0,8},{1,2},{2,1},{3,11},{4,12},{5,6},{6,5},{7,15},{8,0},{9,10},{1... | collective-permute-start | bytes 393224 | tf_op jit(solution)/shard_map/ppermute | solution.py:80
  35.1 5.6 %collective-permute-start.13 = (f32[256,128]{1,0:T(8,128)S(1)}, f32[256,128]{1,0:T(8,128)S(1)}, u32[]{:S(2)}, u32[]{:S(2)}) collective-permute-start(f32[256,128]{1,0:T(8,128)S(1)} %get-tuple-element.76), channel_id=1, source_target_pairs={{0,8},{1,2},{2,1},{3,11},{4,12},{5,6},{6,5},{7,15},{8,0},{9,10},{1... | collective-permute-start | bytes 393224 | tf_op jit(solution)/shard_map/ppermute | solution.py:80
  35.1 6.3 %collective-permute-start.15 = (f32[256,128]{1,0:T(8,128)S(1)}, f32[256,128]{1,0:T(8,128)S(1)}, u32[]{:S(2)}, u32[]{:S(2)}) collective-permute-start(f32[256,128]{1,0:T(8,128)S(1)} %get-tuple-element.78), channel_id=1, source_target_pairs={{0,8},{1,2},{2,1},{3,11},{4,12},{5,6},{6,5},{7,15},{8,0},{9,10},{1... | collective-permute-start | bytes 393224 | tf_op jit(solution)/shard_map/ppermute | solution.py:80
  37.1 6.8 %collective-permute-start.17 = (f32[256,128]{1,0:T(8,128)S(1)}, f32[256,128]{1,0:T(8,128)S(1)}, u32[]{:S(2)}, u32[]{:S(2)}) collective-permute-start(f32[256,128]{1,0:T(8,128)S(1)} %get-tuple-element.80), channel_id=1, source_target_pairs={{0,8},{1,2},{2,1},{3,11},{4,12},{5,6},{6,5},{7,15},{8,0},{9,10},{1... | collective-permute-start | bytes 393224 | tf_op jit(solution)/shard_map/ppermute | solution.py:80
  38.1 20.5 %collective-permute-start.12 = (f32[2,256,128]{2,1,0:T(8,128)S(1)}, f32[2,256,128]{2,1,0:T(8,128)S(1)}, u32[]{:S(2)}, u32[]{:S(2)}) collective-permute-start(f32[2,256,128]{2,1,0:T(8,128)S(1)} %shard_map.107.y_send), channel_id=1, source_target_pairs={{0,4},{1,5},{2,6},{3,7},{4,0},{5,1},{6,2},{7,3},{8,12},{9,13},{10,... | collective-permute-start | bytes 786440 | tf_op jit(solution)/shard_map/ppermute | solution.py:80
  40.7 18.0 %collective-permute-start.14 = (f32[2,256,128]{2,1,0:T(8,128)S(1)}, f32[2,256,128]{2,1,0:T(8,128)S(1)}, u32[]{:S(2)}, u32[]{:S(2)}) collective-permute-start(f32[2,256,128]{2,1,0:T(8,128)S(1)} %shard_map.109.y_send), channel_id=1, source_target_pairs={{0,2},{1,3},{2,0},{3,1},{4,8},{5,9},{6,10},{7,11},{8,4},{9,5},{10,... | collective-permute-start | bytes 786440 | tf_op jit(solution)/shard_map/ppermute | solution.py:80
  41.5 21.8 %collective-permute-start.16 = (f32[2,256,128]{2,1,0:T(8,128)S(1)}, f32[2,256,128]{2,1,0:T(8,128)S(1)}, u32[]{:S(2)}, u32[]{:S(2)}) collective-permute-start(f32[2,256,128]{2,1,0:T(8,128)S(1)} %shard_map.111.y_send), channel_id=1, source_target_pairs={{0,4},{1,5},{2,6},{3,7},{4,0},{5,1},{6,2},{7,3},{8,12},{9,13},{10,... | collective-permute-start | bytes 786440 | tf_op jit(solution)/shard_map/ppermute | solution.py:80
  43.9 19.5 %collective-permute-start.18 = (f32[2,256,128]{2,1,0:T(8,128)S(1)}, f32[2,256,128]{2,1,0:T(8,128)S(1)}, u32[]{:S(2)}, u32[]{:S(2)}) collective-permute-start(f32[2,256,128]{2,1,0:T(8,128)S(1)} %shard_map.113.y_send), channel_id=1, source_target_pairs={{0,2},{1,3},{2,0},{3,1},{4,8},{5,9},{6,10},{7,11},{8,4},{9,5},{10,... | collective-permute-start | bytes 786440 | tf_op jit(solution)/shard_map/ppermute | solution.py:80
  63.5 10.3 %collective-permute-start.19 = (f32[2,2,256,128]{3,2,1,0:T(8,128)S(1)}, f32[2,2,256,128]{3,2,1,0:T(8,128)S(1)}, u32[]{:S(2)}, u32[]{:S(2)}) collective-permute-start(f32[2,2,256,128]{3,2,1,0:T(8,128)S(1)} %shard_map.115), channel_id=1, source_target_pairs={{0,1},{1,0},{2,3},{3,2},{4,5},{5,4},{6,7},{7,6},{8,9},{9,8},{10,11... | collective-permute-start | bytes 1572872 | tf_op jit(solution)/shard_map/ppermute | solution.py:80
  63.6 5.4 %collective-permute-start.20 = (f32[256,128]{1,0:T(8,128)S(1)}, f32[256,128]{1,0:T(8,128)S(1)}, u32[]{:S(2)}, u32[]{:S(2)}) collective-permute-start(f32[256,128]{1,0:T(8,128)S(1)} %get-tuple-element.82), channel_id=1, source_target_pairs={{0,8},{1,2},{2,1},{3,11},{4,12},{5,6},{6,5},{7,15},{8,0},{9,10},{1... | collective-permute-start | bytes 393224 | tf_op jit(solution)/shard_map/ppermute | solution.py:80
  66.0 5.0 %collective-permute-start.21 = (f32[256,128]{1,0:T(8,128)S(1)}, f32[256,128]{1,0:T(8,128)S(1)}, u32[]{:S(2)}, u32[]{:S(2)}) collective-permute-start(f32[256,128]{1,0:T(8,128)S(1)} %get-tuple-element.83), channel_id=1, source_target_pairs={{0,8},{1,2},{2,1},{3,11},{4,12},{5,6},{6,5},{7,15},{8,0},{9,10},{1... | collective-permute-start | bytes 393224 | tf_op jit(solution)/shard_map/ppermute | solution.py:80
  66.1 6.3 %collective-permute-start.22 = (f32[256,128]{1,0:T(8,128)S(1)}, f32[256,128]{1,0:T(8,128)S(1)}, u32[]{:S(2)}, u32[]{:S(2)}) collective-permute-start(f32[256,128]{1,0:T(8,128)S(1)} %get-tuple-element.84), channel_id=1, source_target_pairs={{0,8},{1,2},{2,1},{3,11},{4,12},{5,6},{6,5},{7,15},{8,0},{9,10},{1... | collective-permute-start | bytes 393224 | tf_op jit(solution)/shard_map/ppermute | solution.py:80
  68.1 5.8 %collective-permute-start.23 = (f32[256,128]{1,0:T(8,128)S(1)}, f32[256,128]{1,0:T(8,128)S(1)}, u32[]{:S(2)}, u32[]{:S(2)}) collective-permute-start(f32[256,128]{1,0:T(8,128)S(1)} %get-tuple-element.85), channel_id=1, source_target_pairs={{0,8},{1,2},{2,1},{3,11},{4,12},{5,6},{6,5},{7,15},{8,0},{9,10},{1... | collective-permute-start | bytes 393224 | tf_op jit(solution)/shard_map/ppermute | solution.py:80
  81.2 15.5 %copy-start = (f32[2,4,512,128]{3,2,1,0:T(8,128)}, f32[2,4,512,128]{3,2,1,0:T(8,128)S(1)}, u32[]{:S(2)}) copy-start(f32[2,4,512,128]{3,2,1,0:T(8,128)S(1)} %get-tuple-element.88.accum) | copy-start | bytes 6291460
  81.2 22.3 %copy-start.2 = (f32[2,512,128]{2,1,0:T(8,128)}, f32[2,512,128]{2,1,0:T(8,128)S(1)}, u32[]{:S(2)}) copy-start(f32[2,512,128]{2,1,0:T(8,128)S(1)} %get-tuple-element.90) | copy-start | bytes 1572868
  81.2 22.3 %copy-start.3 = (f32[2,512,128]{2,1,0:T(8,128)}, f32[2,512,128]{2,1,0:T(8,128)S(1)}, u32[]{:S(2)}) copy-start(f32[2,512,128]{2,1,0:T(8,128)S(1)} %get-tuple-element.89) | copy-start | bytes 1572868
  81.3 2.0 %collective-permute-start.28 = (f32[1024,128]{1,0:T(8,128)S(1)}, f32[1024,128]{1,0:T(8,128)S(1)}, u32[]{:S(2)}, u32[]{:S(2)}) collective-permute-start(f32[1024,128]{1,0:T(8,128)S(1)} %bitcast.15), channel_id=1, source_target_pairs={{0,1},{1,0},{2,3},{3,2},{4,5},{5,4},{6,7},{7,6},{8,9},{9,8},{10,11... | collective-permute-start | bytes 1572872 | tf_op jit(solution)/shard_map/ppermute | solution.py:391
  96.8 5.9 %collective-permute-start.29 = (f32[128,128]{1,0:T(8,128)S(1)}, f32[128,128]{1,0:T(8,128)S(1)}, u32[]{:S(2)}, u32[]{:S(2)}) collective-permute-start(f32[128,128]{1,0:T(8,128)S(1)} %shard_map.120.left), channel_id=1, source_target_pairs={{0,16},{1,17},{2,18},{3,19},{4,20},{5,21},{6,22},{7,23},{8,24},{9,... | collective-permute-start | bytes 196616 | tf_op jit(solution)/shard_map/ppermute | solution.py:391
  103.5 11.2 %all-to-all-start.1 = ((f32[8,128,128]{2,1,0:T(8,128)}), f32[8,128,128]{2,1,0:T(8,128)S(1)}, u32[]{:S(2)}, u32[]{:S(2)}) async-start(f32[8,128,128]{2,1,0:T(8,128)} %bitcast.5), calls=%async_computation.1 | async-start | bytes 1048576 | tf_op jit(solution)/shard_map/all_to_all | solution.py:401
  107.0 7.7 %collective-permute-start.24 = (f32[2,512,128]{2,1,0:T(8,128)}, f32[2,512,128]{2,1,0:T(8,128)S(1)}, u32[]{:S(2)}, u32[]{:S(2)}) collective-permute-start(f32[2,512,128]{2,1,0:T(8,128)} %copy-done.3), channel_id=1, source_target_pairs={{0,1},{1,0},{2,3},{3,2},{4,5},{5,4},{6,7},{7,6},{8,9},{9,8},{10,11... | collective-permute-start | bytes 1572872 | tf_op jit(solution)/shard_map/ppermute | solution.py:80
  107.1 12.1 %collective-permute-start.25 = (f32[2,512,128]{2,1,0:T(8,128)}, f32[2,512,128]{2,1,0:T(8,128)}, u32[]{:S(2)}, u32[]{:S(2)}) collective-permute-start(f32[2,512,128]{2,1,0:T(8,128)} %copy-done.2), channel_id=1, source_target_pairs={{0,4},{1,2},{2,1},{3,7},{4,0},{5,6},{6,5},{7,3},{8,12},{9,10},{10,... | collective-permute-start | bytes 1572872 | tf_op jit(solution)/shard_map/ppermute | solution.py:80
  114.7 21.0 %collective-permute-start.30 = (f32[1024,128]{1,0:T(8,128)S(1)}, f32[1024,128]{1,0:T(8,128)S(1)}, u32[]{:S(2)}, u32[]{:S(2)}) collective-permute-start(f32[1024,128]{1,0:T(8,128)S(1)} %bitcast.11), channel_id=1, source_target_pairs={{0,1},{1,0},{2,3},{3,2},{4,5},{5,4},{6,7},{7,6},{8,9},{9,8},{10,11... | collective-permute-start | bytes 1572872 | tf_op jit(solution)/shard_map/ppermute | solution.py:391
  119.2 1.6 %copy-start.1 = (f32[2,4,512,128]{3,2,1,0:T(8,128)S(1)}, f32[2,4,512,128]{3,2,1,0:T(8,128)}, u32[]{:S(2)}) copy-start(f32[2,4,512,128]{3,2,1,0:T(8,128)} %copy-done) | copy-start | bytes 6291460
  122.0 12.9 %collective-permute-start.26 = (f32[2,2,128,128]{3,2,1,0:T(8,128)S(1)}, f32[2,2,128,128]{3,2,1,0:T(8,128)S(1)}, u32[]{:S(2)}, u32[]{:S(2)}) collective-permute-start(f32[2,2,128,128]{3,2,1,0:T(8,128)S(1)} %get-tuple-element.92), channel_id=1, source_target_pairs={{0,4},{1,5},{2,6},{3,7},{4,0},{5,1},{6,2},{7,3},{8,12},{9,13},{10,... | collective-permute-start | bytes 786440 | tf_op jit(solution)/shard_map/ppermute | solution.py:80
  123.4 11.5 %collective-permute-start.27 = (f32[2,2,128,128]{3,2,1,0:T(8,128)S(1)}, f32[2,2,128,128]{3,2,1,0:T(8,128)S(1)}, u32[]{:S(2)}, u32[]{:S(2)}) collective-permute-start(f32[2,2,128,128]{3,2,1,0:T(8,128)S(1)} %get-tuple-element.93), channel_id=1, source_target_pairs={{0,2},{1,3},{2,0},{3,1},{4,8},{5,9},{6,10},{7,11},{8,4},{9,5},{10,... | collective-permute-start | bytes 786440 | tf_op jit(solution)/shard_map/ppermute | solution.py:80
where the time goes:
time: 137 us
  waiting for transfers between devices  59.1 us (43%)
  starting transfers between devices  37.5 us (27%)
  Pallas kernels  24.4 us (18%)
  blocking collectives  13.4 us (10%)
  local copies, waits for them, and re-layouts  1.61 us (1%)
    ppermute x28, waiting for transfers between devices, pair_exchange(): return lax.ppermute(block, (SY, SX), perm)  47.4 us
    ppermute x28, starting transfers between devices, pair_exchange(): return lax.ppermute(block, (SY, SX), perm)  32 us
    pallas_call x21, Pallas kernels, call(): pl.pallas_call(kernel, out_shape=out_shape, in_specs=specs, out_specs=jax...  24.4 us
    all_to_all x1, blocking collectives, block_exchange(): lax.all_to_all(pieces, (SY, SX), 0, 0, tiled=True, axis_index_groups=list...  13.4 us
    ppermute x3, waiting for transfers between devices, flip_exchange(): return lax.ppermute(block, (SY, SX), perm)  5.91 us
    all_to_all x1, waiting for transfers between devices, block_exchange(): lax.all_to_all(pieces, (SY, SX), 0, 0, tiled=True, axis_index_groups=list...  5.78 us
    all_to_all x1, starting transfers between devices, block_exchange(): lax.all_to_all(pieces, (SY, SX), 0, 0, tiled=True, axis_index_groups=list...  3.49 us
  transfers between devices with their start and end apart: 32, of which 15 were waited for; matrix products, arithmetic and copies ran while one was open for 0% of the time, Pallas kernels for 4%

commit v1 on v0

--- a/solution.py
+++ b/solution.py
@@ -103,30 +103,44 @@
     return pl.multiple_of(value, unit)
 
 
-def pack_tile_kernel(h, obj_re, obj_im, *outs_and_sems):
-    outs, sems = outs_and_sems[:-1], outs_and_sems[-1]
-    y_even, y_odd, x_even, x_odd, tile = outs[:2], outs[2:4], outs[4], outs[5], outs[6]
-    py, px = parity(SY), parity(SX)
-    copies = []
-    for c, obj in enumerate((obj_re, obj_im)):
-        for out, side in ((y_even[c], 1 - py), (y_odd[c], py)):
-            rows = pl.ds(aligned(side * h, h), h)
-            copies += [(obj.at[rows, pl.ds(lb * h, h)], out.at[lb]) for lb in range(2)]
-        for out, side in ((x_even, 1 - px), (x_odd, px)):
-            copies.append((obj.at[:, pl.ds(aligned(side * h, h), h)], out.at[c]))
-        copies += [(obj.at[:, pl.ds(lb * h, h)], tile.at[c, lb]) for lb in range(2)]
-    copies = [pltpu.make_async_copy(a, b, sems.at[i]) for i, (a, b) in enumerate(copies)]
+def run_copies(pairs, sems):
+    copies = [pltpu.make_async_copy(a, b, sems.at[i]) for i, (a, b) in enumerate(pairs)]
     for copy in copies:
         copy.start()
     for copy in copies:
         copy.wait()
 
 
-def pack_corner_kernel(up_even, up_odd, c_even, c_odd):
+def lane_block(far):
     px = parity(SX)
+    return px if far else 1 - px
+
+
+def pack_rows_kernel(h, obj_re, obj_im, *outs_and_sems):
+    *outs, sems = outs_and_sems
+    py = parity(SY)
+    pairs = []
+    for at, out in enumerate(outs):
+        far, odd = divmod(at, 2)
+        rows = pl.ds(aligned((py if odd else 1 - py) * h, h), h)
+        columns = pl.ds(aligned(lane_block(far) * h, h), h)
+        pairs += [(obj.at[rows, columns], out.at[c]) for c, obj in enumerate((obj_re, obj_im))]
+    run_copies(pairs, sems)
+
+
+def pack_columns_kernel(h, obj_re, obj_im, x_even, x_odd, tile, sems):
+    px = parity(SX)
+    pairs = []
+    for c, obj in enumerate((obj_re, obj_im)):
+        for out, side in ((x_even, 1 - px), (x_odd, px)):
+            pairs.append((obj.at[:, pl.ds(aligned(side * h, h), h)], out.at[c]))
+        pairs += [(obj.at[:, pl.ds(lb * h, h)], tile.at[c, lb]) for lb in range(2)]
+    run_copies(pairs, sems)
+
+
+def pack_corner_kernel(up_even, up_odd, corner):
     for odd, strip in enumerate((up_even, up_odd)):
-        c_even[odd] = masked(SY, odd, strip[1 - px])
-        c_odd[odd] = masked(SY, odd, strip[px])
+        corner[odd] = masked(SY, odd, strip[...])
 
 
 def batch_body(
@@ -190,7 +204,7 @@
                     [field[pl.ds(m * f + r, rows), pl.ds(c * f + lb * h, h)] for c in range(2)] for m in range(2)
                 ]
                 power = sum(part * part for mode in far for part in mode)
-                ratio = amp[j, pl.ds(r, rows), pl.ds(lb * h, h)] * lax.rsqrt(jnp.maximum(power, 1.0))
+                ratio = amp[batch * size + j, pl.ds(r, rows), pl.ds(lb * h, h)] * lax.rsqrt(jnp.maximum(power, 1.0))
                 for m in range(2):
                     for c in range(2):
                         spot = pl.ds(m * f + lb * h, h)
@@ -249,52 +263,39 @@
 
 
 def first_batch_kernel(
-    h, size, order, offs, tile, up_even_re, up_even_im, up_odd_re, up_odd_im, x_even, x_odd,
-    c_even_re, c_even_im, c_odd_re, c_odd_im, probe_re, probe_im, table_left, table_right, amp, amp_hbm,
-    ext, accum, send_even, send_00, send_01, send_10, send_11, grads, amp_next, amp_sems, *scratch,
+    h, size, order, offs, tile, up_00, up_01, up_10, up_11, x_even, x_odd, c_even, c_odd,
+    probe_re, probe_im, table_left, table_right, amp,
+    ext, accum, send_even, send_odd_re, send_odd_im, grads, *scratch,
 ):
     py, px = parity(SY), parity(SX)
-    copies = [
-        pltpu.make_async_copy(amp_hbm.at[0, 0, order[0, 0, size + j]], amp_next.at[j], amp_sems.at[j]) for j in range(size)
-    ]
-    for copy in copies:
-        copy.start()
     halo_rows = [pl.ds(aligned(side * 3 * h, h), h) for side in (1 - py, py)]
-    ups = ((up_even_re, up_odd_re), (up_even_im, up_odd_im))
-    corners = ((c_even_re, c_odd_re), (c_even_im, c_odd_im))
+    ups = ((up_00, up_01), (up_10, up_11))
     for c in range(2):
         for lb in range(2):
             ext[c, 1 + lb, h : 3 * h] = tile[c, lb]
+        for far, (block, column, corner) in enumerate((((1 - px) * 3, x_even, c_even), (px * 3, x_odd, c_odd))):
+            ext[c, block, h : 3 * h] = masked(SX, far, column[c])
             for odd in range(2):
-                ext[c, 1 + lb, halo_rows[odd]] = masked(SY, odd, ups[c][odd][lb])
-        for odd, (block, column) in enumerate((((1 - px) * 3, x_even), (px * 3, x_odd))):
-            ext[c, block, h : 3 * h] = masked(SX, odd, column[c])
-            for odd_row in range(2):
-                ext[c, block, halo_rows[odd_row]] = masked(SX, odd, corners[c][odd][odd_row])
+                ext[c, 1 + lane_block(far), halo_rows[odd]] = masked(SY, odd, ups[far][odd][c])
+                ext[c, block, halo_rows[odd]] = masked(SX, far, corner[odd, c])
     probe, tables = (probe_re, probe_im), (table_left, table_right)
     batch_body(0, size, order, offs, probe, tables, amp, ext, accum, grads, None, scratch)
-    for copy in copies:
-        copy.wait()
-    for c, sends in enumerate(((send_00, send_01), (send_10, send_11))):
+    for c, send_odd in enumerate((send_odd_re, send_odd_im)):
         send_even[c] = accum[c, (1 - px) * 3]
-        for odd, send in enumerate(sends):
-            send[...] = accum[c, px * 3, half_rows(h, odd)]
+        send_odd[...] = accum[c, px * 3]
 
 
 def last_batch_kernel(
-    h, size, batch, order, offs, columns_00, columns_01, columns_10, columns_11, x_even, odd_00, odd_01, odd_10, odd_11,
-    grads_in, probe_re, probe_im, table_left, table_right, amp, accum, send_even, send_odd, keep, give, ext, grads, *scratch,
+    size, batch, order, offs, near_re, near_im, far_re, far_im, even_re, even_im, odd_re, odd_im, grads_in,
+    probe_re, probe_im, table_left, table_right, amp, accum, send_even, send_odd, keep, give, ext, grads, *scratch,
 ):
     px = parity(SX)
-    columns = ((columns_00, columns_01), (columns_10, columns_11))
-    x_odd = ((odd_00, odd_01), (odd_10, odd_11))
-    for c in range(2):
-        for odd in range(2):
-            rows = half_rows(h, odd)
-            for lb in range(2):
-                ext[c, 1 + lb, rows] = columns[c][odd][lb]
-            ext[c, (1 - px) * 3, rows] = masked(SX, 0, x_even[c, odd])
-            ext[c, px * 3, rows] = masked(SX, 1, x_odd[c][odd][...])
+    for c, parts in enumerate(((near_re, far_re, even_re, odd_re), (near_im, far_im, even_im, odd_im))):
+        near, far, x_even, x_odd = parts
+        ext[c, 1 + lane_block(0)] = near[...]
+        ext[c, 1 + lane_block(1)] = far[...]
+        ext[c, (1 - px) * 3] = masked(SX, 0, x_even[...])
+        ext[c, px * 3] = masked(SX, 1, x_odd[...])
     probe, tables = (probe_re, probe_im), (table_left, table_right)
     batch_body(batch, size, order, offs, probe, tables, amp, ext, accum, grads, grads_in, scratch)
     keep[...] = grads[px]
@@ -319,58 +320,46 @@
     return pl.ds(aligned(half_side(odd) * 2 * h, 2 * h), 2 * h)
 
 
-def fold_columns_kernel(h, c, odd, accum, x_even, x_odd, y_send):
-    px = parity(SX)
-    rows = half_rows(h, odd)
-    columns = masked(SX, 0, x_even[c, rows]), masked(SX, 1, x_odd[...])
-    for block, column in zip((1 - px, px), columns):
-        y_send[block] = accum[c, 1 + block, rows] + column
-
-
-def update_kernel(h, c, odd, scale, y_send, y_got, ext, columns, x_send):
-    px, side = parity(SX), half_side(odd)
+def fold_columns_kernel(h, c, far, accum, x_got, y_even, y_odd):
+    for odd, y_send in enumerate((y_even, y_odd)):
+        rows = half_rows(h, odd)
+        column = x_got[rows] if far else x_got[c, rows]
+        y_send[...] = accum[c, 1 + lane_block(far), rows] + masked(SX, far, column)
+
+
+def update_kernel(h, c, far, scale, sent_even, got_even, sent_odd, got_odd, ext, columns):
     rate = scale[0:1, :]
-    rate_halo = jnp.where(has_partner(SY, odd), rate, 0.0)
-    for lb in range(2):
+    for odd, sent, got in ((0, sent_even, got_even), (1, sent_odd, got_odd)):
+        side = half_side(odd)
+        rate_halo = jnp.where(has_partner(SY, odd), rate, 0.0)
         for at, factor in ((1 - side, rate), (side, rate_halo)):
             here = pl.ds(aligned(at * h, h), h)
             there = pl.ds(aligned((2 * side + at) * h, h), h)
-            total = y_send[lb, here] + masked(SY, odd, y_got[lb, here])
-            columns[lb, here] = ext[c, 1 + lb, there] + factor * total
-    x_send[...] = columns[px]
-
-
-def pack_even_kernel(columns_00, columns_01, columns_10, columns_11, x_even):
-    px = parity(SX)
-    for c, parts in enumerate(((columns_00, columns_01), (columns_10, columns_11))):
-        for odd, part in enumerate(parts):
-            x_even[c, odd] = part[1 - px]
+            total = sent[here] + masked(SY, odd, got[here])
+            columns[there] = ext[c, 1 + lane_block(far), there] + factor * total
 
 
 def fold_last_kernel(h, accum, x_even, x_odd, inner, y_even, y_odd):
-    py, px = parity(SY), parity(SX)
-    for c in range(2):
-        columns = masked(SX, 0, x_even[c]), masked(SX, 1, x_odd[c])
-        for block, column in zip((1 - px, px), columns):
-            total = accum[c, 1 + block] + column
-            inner[c, block] = total[h : 3 * h]
-            y_even[c, block] = jnp.where(py == 0, total[3 * h :], total[:h])
-            y_odd[c, block] = jnp.where(py == 0, total[:h], total[3 * h :])
-
-
-def finish_object_kernel(
-    h, scale, inner, y_even, y_odd, columns_00, columns_01, columns_10, columns_11, out_re, out_im
-):
+    py = parity(SY)
+    for far, x_got in enumerate((x_even, x_odd)):
+        for c in range(2):
+            total = accum[c, 1 + lane_block(far)] + masked(SX, far, x_got[c])
+            inner[far, c] = total[h : 3 * h]
+            y_even[far, c] = jnp.where(py == 0, total[3 * h :], total[:h])
+            y_odd[far, c] = jnp.where(py == 0, total[:h], total[3 * h :])
+
+
+def finish_object_kernel(h, scale, inner, y_even, y_odd, near_re, near_im, far_re, far_im, *outs):
+    columns = (near_re, near_im), (far_re, far_im)
     rate = scale[0:1, :]
-    columns = ((columns_00, columns_01), (columns_10, columns_11))
-    for c, out in enumerate((out_re, out_im)):
-        for lb in range(2):
+    for far in range(2):
+        lanes = pl.ds(aligned(lane_block(far) * h, h), h)
+        for c, out in enumerate(outs):
             for odd, got in enumerate((y_even, y_odd)):
                 side = half_side(odd)
                 here = pl.ds(aligned(side * h, h), h)
-                old = columns[c][odd][lb, pl.ds(aligned((1 - side) * h, h), h)]
-                total = inner[c, lb, here] + masked(SY, odd, got[c, lb])
-                out[here, lb * h : (lb + 1) * h] = old + rate * total
+                old = columns[far][c][pl.ds(aligned((1 + side) * h, h), h)]
+                out[here, lanes] = old + rate * (inner[far, c, here] + masked(SY, odd, got[far, c]))
 
 
 def plan_bits():
@@ -439,74 +428,70 @@
     arrays = (visit_order, offsets, probe_re, probe_im)
     table_left, table_right, scale, *arrays, amp = call(
         prepare_kernel,
-        [table_type, table_type, f32(8, h)] + [jax.ShapeDtypeStruct(a.shape, a.dtype) for a in arrays] + [f32(size, f, f)],
+        [table_type, table_type, f32(8, h)] + [jax.ShapeDtypeStruct(a.shape, a.dtype) for a in arrays] + [f32(positions, f, f)],
         (visit_order, *map(in_hbm, arrays), in_hbm(amplitudes)),
         [SMEM] + [HBM] * 5,
-        [pltpu.SemaphoreType.DMA((4 + size,))],
+        [pltpu.SemaphoreType.DMA((4 + positions,))],
     )
     visit_order, offsets, *probe = arrays
     strip = f32(2, h, h)
     block = f32(2, 2 * h, h)
-    up = call(
-        functools.partial(pack_tile_kernel, h),
-        [strip] * 4 + [block] * 2 + [f32(2, 2, 2 * h, h)],
-        (in_hbm(object_re), in_hbm(object_im)),
-        [HBM] * 2,
-        [pltpu.SemaphoreType.DMA((16,))],
-    )
-    up_even = [pair_exchange(up[c], SY, 0) for c in range(2)]
-    up_odd = [pair_exchange(up[2 + c], SY, 1) for c in range(2)]
-    x_even = pair_exchange(up[4], SX, 0)
-    x_odd = pair_exchange(up[5], SX, 1)
-    corners = [call(pack_corner_kernel, [strip, strip], (up_even[c], up_odd[c])) for c in range(2)]
-    c_even = [pair_exchange(corners[c][0], SX, 0) for c in range(2)]
-    c_odd = [pair_exchange(corners[c][1], SX, 1) for c in range(2)]
-
-    column, columns_type = f32(2 * h, h), f32(2, 4 * h, h)
+    objects = in_hbm(object_re), in_hbm(object_im)
+    sems = [pltpu.SemaphoreType.DMA((8,))]
+    up = call(functools.partial(pack_rows_kernel, h), [strip] * 4, objects, [HBM] * 2, sems)
+    x_even, x_odd, tile = call(
+        functools.partial(pack_columns_kernel, h), [block, block, f32(2, 2, 2 * h, h)], objects, [HBM] * 2, sems
+    )
+    ups = {}
+    for far in (1, 0):
+        ups[far] = [pair_exchange(up[2 * far + odd], SY, odd) for odd in range(2)]
+    x_even = pair_exchange(x_even, SX, 0)
+    x_odd = pair_exchange(x_odd, SX, 1)
+    corners = [pair_exchange(call(pack_corner_kernel, f32(2, 2, h, h), ups[far]), SX, far) for far in range(2)]
+
+    column, columns_type = f32(4 * h, h), f32(2, 4 * h, h)
     ext_type, grads_type = f32(2, 4, 4 * h, h), f32(2, 2, 2, f, h)
     fixed_args = (*probe, table_left, table_right)
     fixed_specs = [VMEM] * 4
-    ext, accum, send_even, *send_odd, grads, amp_next = call(
+    ext, accum, send_even, *send_odd, grads = call(
         functools.partial(first_batch_kernel, h, size),
-        [ext_type, ext_type, columns_type] + [column] * 4 + [grads_type, f32(size, f, f)],
-        (visit_order, offsets, up[6], *up_even, *up_odd, x_even, x_odd, *c_even, *c_odd, *fixed_args, amp, in_hbm(amplitudes)),
-        [SMEM] * 2 + [VMEM] * 12 + fixed_specs + [HBM],
-        [pltpu.SemaphoreType.DMA((size,)), *batch_scratch(f)],
+        [ext_type, ext_type, columns_type, column, column, grads_type],
+        (visit_order, offsets, tile, *ups[0], *ups[1], x_even, x_odd, *corners, *fixed_args, amp),
+        [SMEM] * 2 + [VMEM] * 10 + fixed_specs,
+        batch_scratch(f),
         9 << 20,
     )
 
-    streams = [(c, odd) for c in range(2) for odd in range(2)]
+    half = f32(2 * h, h)
     x_even = pair_exchange(send_even, SX, 0)
-    columns, x_odd = [], []
-    for (c, odd), part in zip(streams, send_odd):
-        x_got = pair_exchange(part, SX, 1)
-        y_send = call(functools.partial(fold_columns_kernel, h, c, odd), block, (accum, x_even, x_got))
-        y_got = pair_exchange(y_send, SY, odd)
-        new, x_send = call(functools.partial(update_kernel, h, c, odd), [block, column], (scale, y_send, y_got, ext))
-        columns.append(new)
-        x_odd.append(pair_exchange(x_send, SX, 1))
-    x_send = call(pack_even_kernel, f32(2, 2, 2 * h, h), columns)
-    x_even = pair_exchange(x_send, SX, 0)
+    x_odd = [pair_exchange(part, SX, 1) for part in send_odd]
+    columns, halos = {}, {}
+    for far, c in ((0, 0), (1, 0), (1, 1), (0, 1)):
+        sent = call(
+            functools.partial(fold_columns_kernel, h, c, far), [half, half], (accum, x_odd[c] if far else x_even)
+        )
+        got = [pair_exchange(part, SY, odd) for odd, part in enumerate(sent)]
+        columns[far, c] = call(
+            functools.partial(update_kernel, h, c, far), column, (scale, sent[0], got[0], sent[1], got[1], ext)
+        )
+        halos[far, c] = pair_exchange(columns[far, c], SX, far)
+    columns, halos = [[table[far, c] for far in range(2) for c in range(2)] for table in (columns, halos)]
     modes = f32(2, 2, f, h)
     accum, send_even, send_odd, keep, give = call(
-        functools.partial(last_batch_kernel, h, size, 1),
+        functools.partial(last_batch_kernel, size, 1),
         [ext_type, columns_type, columns_type, modes, modes],
-        (visit_order, offsets, *columns, x_even, *x_odd, grads, *fixed_args, amp_next),
-        [SMEM] * 2 + [VMEM] * 11 + fixed_specs,
+        (visit_order, offsets, *columns, *halos, grads, *fixed_args, amp),
+        [SMEM] * 2 + [VMEM] * 10 + fixed_specs,
         [pltpu.VMEM(t.shape, t.dtype) for t in (ext_type, grads_type)] + batch_scratch(f),
         12 << 20,
     )
 
-    x_odd = pair_exchange(send_odd, SX, 1, 1)
-    x_even = pair_exchange(send_even, SX, 0)
-    last = f32(2, 2, h, h)
-    inner, y_even, y_odd = call(
-        functools.partial(fold_last_kernel, h), [f32(2, 2, 2 * h, h), last, last], (accum, x_even, x_odd)
-    )
-    y_even = pair_exchange(y_even, SY, 0)
-    y_odd = pair_exchange(y_odd, SY, 1)
+    x_got = pair_exchange(send_even, SX, 0), pair_exchange(send_odd, SX, 1, 1)
+    strips = f32(2, 2, h, h)
+    inner, *sent = call(functools.partial(fold_last_kernel, h), [f32(2, 2, 2 * h, h), strips, strips], (accum, *x_got))
+    got = [pair_exchange(part, SY, odd) for odd, part in enumerate(sent)]
     out_re, out_im = call(
-        functools.partial(finish_object_kernel, h), [f32(2 * h, 2 * h)] * 2, (scale, inner, y_even, y_odd, *columns)
+        functools.partial(finish_object_kernel, h), [f32(2 * h, 2 * h)] * 2, (scale, inner, *got, *columns)
     )
 
     first, block_bits, pairs = plan_bits()

time: 137 us -> 131 us (0.956)
  waiting for transfers between devices: 59.1 us -> 47.4 us
  starting transfers between devices: 37.5 us -> 42.2 us
    ppermute x28 -> x27, waiting for transfers between devices: 47.4 us -> 35.6 us  [pair_exchange(): return lax.ppermute(block, (SY, SX), perm)]
    ppermute x28 -> x27, starting transfers between devices: 32 us -> 36.9 us  [pair_exchange(): return lax.ppermute(block, (SY, SX), perm)]
  transfers between devices with their start and end apart: 32 -> 31, of which waited for: 15 -> 13; matrix products, arithmetic and copies ran while one was open for 0% -> 0% of each run, Pallas kernels for 4% -> 5%
where the time goes in v1:
time: 131 us
  waiting for transfers between devices  47.4 us (36%)
  starting transfers between devices  42.2 us (32%)
  Pallas kernels  24.5 us (19%)
  blocking collectives  14.3 us (11%)
  local copies, waits for them, and re-layouts  1.61 us (1%)
    ppermute x27, starting transfers between devices, pair_exchange(): return lax.ppermute(block, (SY, SX), perm)  36.9 us
    ppermute x27, waiting for transfers between devices, pair_exchange(): return lax.ppermute(block, (SY, SX), perm)  35.6 us
    pallas_call x21, Pallas kernels, call(): pl.pallas_call(kernel, out_shape=out_shape, in_specs=specs, out_specs=jax...  24.5 us
    all_to_all x1, blocking collectives, block_exchange(): lax.all_to_all(pieces, (SY, SX), 0, 0, tiled=True, axis_index_groups=list...  14.3 us
    ppermute x3, waiting for transfers between devices, flip_exchange(): return lax.ppermute(block, (SY, SX), perm)  6.09 us
    all_to_all x1, waiting for transfers between devices, block_exchange(): lax.all_to_all(pieces, (SY, SX), 0, 0, tiled=True, axis_index_groups=list...  5.78 us
    all_to_all x1, starting transfers between devices, block_exchange(): lax.all_to_all(pieces, (SY, SX), 0, 0, tiled=True, axis_index_groups=list...  3.49 us
  transfers between devices with their start and end apart: 31, of which 13 were waited for; matrix products, arithmetic and copies ran while one was open for 0% of the time, Pallas kernels for 5%

profile of v1, /device:TPU:0, one launch (start us, length us, event | category | flops | bytes accessed | tf_op | source)
XLA Modules:
  0.0 130.9 jit_solution(2065056390864609034)
XLA Ops:
  0.6 1.1 shard_map.104
  1.8 3.1 %collective-permute-start = (f32[2,128,128]{2,1,0:T(8,128)S(1)}, f32[2,128,128]{2,1,0:T(8,128)S(1)}, u32[]{:S(2)}, u32[]{:S(2)}) collective-permute-start(f32[2,128,128]{2,1,0:T(8,128)S(1)} %get-tuple-element.49), channel_id=1, source_target_pairs={{0,4},{1,5},{2,6},{3,7},{4,0},{5,1},{6,2},{7,3},{8,12},{9,13},{10,... | collective-permute-start | bytes 393224 | tf_op jit(solution)/shard_map/ppermute | solution.py:80
  4.8 1.5 %collective-permute-start.1 = (f32[2,128,128]{2,1,0:T(8,128)S(1)}, f32[2,128,128]{2,1,0:T(8,128)S(1)}, u32[]{:S(2)}, u32[]{:S(2)}) collective-permute-start(f32[2,128,128]{2,1,0:T(8,128)S(1)} %get-tuple-element.50), channel_id=1, source_target_pairs={{0,2},{1,3},{2,0},{3,1},{4,8},{5,9},{6,10},{7,11},{8,4},{9,5},{10,... | collective-permute-start | bytes 393224 | tf_op jit(solution)/shard_map/ppermute | solution.py:80
  6.3 1.5 %collective-permute-start.2 = (f32[2,128,128]{2,1,0:T(8,128)S(1)}, f32[2,128,128]{2,1,0:T(8,128)S(1)}, u32[]{:S(2)}, u32[]{:S(2)}) collective-permute-start(f32[2,128,128]{2,1,0:T(8,128)S(1)} %get-tuple-element.51), channel_id=1, source_target_pairs={{0,4},{1,5},{2,6},{3,7},{4,0},{5,1},{6,2},{7,3},{8,12},{9,13},{10,... | collective-permute-start | bytes 393224 | tf_op jit(solution)/shard_map/ppermute | solution.py:80
  7.9 1.5 %collective-permute-start.3 = (f32[2,128,128]{2,1,0:T(8,128)S(1)}, f32[2,128,128]{2,1,0:T(8,128)S(1)}, u32[]{:S(2)}, u32[]{:S(2)}) collective-permute-start(f32[2,128,128]{2,1,0:T(8,128)S(1)} %get-tuple-element.52), channel_id=1, source_target_pairs={{0,2},{1,3},{2,0},{3,1},{4,8},{5,9},{6,10},{7,11},{8,4},{9,5},{10,... | collective-permute-start | bytes 393224 | tf_op jit(solution)/shard_map/ppermute | solution.py:80
  9.4 1.3 %shard_map.103 = (f32[2,256,128]{2,1,0:T(8,128)S(1)}, f32[2,256,128]{2,1,0:T(8,128)S(1)}, f32[2,2,256,128]{3,2,1,0:T(8,128)S(1)}) custom-call(f32[256,256]{1,0:T(8,128)} %obj_re.3, f32[256,256]{1,0:T(8,128)} %obj_im.3), custom_call_target="tpu_custom_call" | custom-call | tf_op jit(solution)/shard_map/pallas_call | solution.py:27
  10.8 3.5 %collective-permute-done.up_even.up_00 = f32[2,128,128]{2,1,0:T(8,128)S(1)} collective-permute-done((f32[2,128,128]{2,1,0:T(8,128)S(1)}, f32[2,128,128]{2,1,0:T(8,128)S(1)}, u32[]{:S(2)}, u32[]{:S(2)}) %collective-permute-start) | collective-permute-done | bytes 131104 | tf_op jit(solution)/shard_map/ppermute | solution.py:80
  14.3 2.0 %collective-permute-start.5 = (f32[2,256,128]{2,1,0:T(8,128)S(1)}, f32[2,256,128]{2,1,0:T(8,128)S(1)}, u32[]{:S(2)}, u32[]{:S(2)}) collective-permute-start(f32[2,256,128]{2,1,0:T(8,128)S(1)} %get-tuple-element.54), channel_id=1, source_target_pairs={{0,8},{1,2},{2,1},{3,11},{4,12},{5,6},{6,5},{7,15},{8,0},{9,10},{1... | collective-permute-start | bytes 786440 | tf_op jit(solution)/shard_map/ppermute | solution.py:80
  16.5 2.1 %collective-permute-start.7 = (f32[2,2,128,128]{3,2,1,0:T(8,128)S(1)}, f32[2,2,128,128]{3,2,1,0:T(8,128)S(1)}, u32[]{:S(2)}, u32[]{:S(2)}) collective-permute-start(f32[2,2,128,128]{3,2,1,0:T(8,128)S(1)} %shard_map.106), channel_id=1, source_target_pairs={{0,8},{1,2},{2,1},{3,11},{4,12},{5,6},{6,5},{7,15},{8,0},{9,10},{1... | collective-permute-start | bytes 786440 | tf_op jit(solution)/shard_map/ppermute | solution.py:80
  18.7 2.8 %shard_map.102 = (bf16[512,512]{1,0:T(8,128)(2,1)S(1)}, bf16[512,512]{1,0:T(8,128)(2,1)S(1)}, f32[8,128]{1,0:T(8,128)S(1)}, s32[1,1,8]{2,1,0:T(1,128)S(1)}, s32[...) custom-call(s32[1,1,8]{2,1,0:T(1,128)} %order_hbm.1, ...), custom_call_target="tpu_custom_call" | custom-call | tf_op jit(solution)/shard_map/pallas_call | solution.py:27
  21.6 2.0 %collective-permute-done.7.c_odd = f32[2,2,128,128]{3,2,1,0:T(8,128)S(1)} collective-permute-done((f32[2,2,128,128]{3,2,1,0:T(8,128)S(1)}, f32[2,2,128,128]{3,2,1,0:T(8,128)S(1)}, u32[]{:S(2)}, u32[]{:S(2)}) %collective-permute-start.7) | collective-permute-done | bytes 262176 | tf_op jit(solution)/shard_map/ppermute | solution.py:80
  23.5 7.1 %shard_map.107 = (f32[2,4,512,128]{3,2,1,0:T(8,128)S(1)}, f32[2,4,512,128]{3,2,1,0:T(8,128)S(1)}, f32[2,512,128]{2,1,0:T(8,128)S(1)}, f32[512,128]{1,0:T(8,128)S...) custom-call(s32[1,1,8]{2,1,0:T(1,128)S(1)} %get-tuple-element.46.order, ...), custom_call_target="tpu_custom_call" | custom-call | tf_op jit(solution)/shard_map/pallas_call | solution.py:27
  30.7 2.1 %collective-permute-start.13 = (f32[512,128]{1,0:T(8,128)S(1)}, f32[512,128]{1,0:T(8,128)S(1)}, u32[]{:S(2)}, u32[]{:S(2)}) collective-permute-start(f32[512,128]{1,0:T(8,128)S(1)} %get-tuple-element.67), channel_id=1, source_target_pairs={{0,8},{1,2},{2,1},{3,11},{4,12},{5,6},{6,5},{7,15},{8,0},{9,10},{1... | collective-permute-start | bytes 786440 | tf_op jit(solution)/shard_map/ppermute | solution.py:80
  32.9 0.1 collective-permute-start.16
  33.0 4.3 %collective-permute-done.13.x_got = f32[512,128]{1,0:T(8,128)S(1)} collective-permute-done((f32[512,128]{1,0:T(8,128)S(1)}, f32[512,128]{1,0:T(8,128)S(1)}, u32[]{:S(2)}, u32[]{:S(2)}) %collective-permute-start.13) | collective-permute-done | bytes 262176 | tf_op jit(solution)/shard_map/ppermute | solution.py:80
  37.3 2.6 %collective-permute-start.14 = (f32[256,128]{1,0:T(8,128)S(1)}, f32[256,128]{1,0:T(8,128)S(1)}, u32[]{:S(2)}, u32[]{:S(2)}) collective-permute-start(f32[256,128]{1,0:T(8,128)S(1)} %get-tuple-element.68.sent_even), channel_id=1, source_target_pairs={{0,4},{1,5},{2,6},{3,7},{4,0},{5,1},{6,2},{7,3},{8,12},{9,13},{10,... | collective-permute-start | bytes 393224 | tf_op jit(solution)/shard_map/ppermute | solution.py:80
  39.8 0.2 collective-permute-start.15
  40.1 2.9 %collective-permute-start.17 = (f32[256,128]{1,0:T(8,128)S(1)}, f32[256,128]{1,0:T(8,128)S(1)}, u32[]{:S(2)}, u32[]{:S(2)}) collective-permute-start(f32[256,128]{1,0:T(8,128)S(1)} %get-tuple-element.71.sent_even), channel_id=1, source_target_pairs={{0,4},{1,5},{2,6},{3,7},{4,0},{5,1},{6,2},{7,3},{8,12},{9,13},{10,... | collective-permute-start | bytes 393224 | tf_op jit(solution)/shard_map/ppermute | solution.py:80
  43.0 0.4 collective-permute-start.18
  43.4 2.7 %collective-permute-start.9 = (f32[256,128]{1,0:T(8,128)S(1)}, f32[256,128]{1,0:T(8,128)S(1)}, u32[]{:S(2)}, u32[]{:S(2)}) collective-permute-start(f32[256,128]{1,0:T(8,128)S(1)} %get-tuple-element.62.sent_even), channel_id=1, source_target_pairs={{0,4},{1,5},{2,6},{3,7},{4,0},{5,1},{6,2},{7,3},{8,12},{9,13},{10,... | collective-permute-start | bytes 393224 | tf_op jit(solution)/shard_map/ppermute | solution.py:80
  46.2 3.1 %collective-permute-done.14.got_even = f32[256,128]{1,0:T(8,128)S(1)} collective-permute-done((f32[256,128]{1,0:T(8,128)S(1)}, f32[256,128]{1,0:T(8,128)S(1)}, u32[]{:S(2)}, u32[]{:S(2)}) %collective-permute-start.14) | collective-permute-done | bytes 131104 | tf_op jit(solution)/shard_map/ppermute | solution.py:80
  49.3 0.2 collective-permute-start.10
  49.6 3.1 %collective-permute-start.11 = (f32[256,128]{1,0:T(8,128)S(1)}, f32[256,128]{1,0:T(8,128)S(1)}, u32[]{:S(2)}, u32[]{:S(2)}) collective-permute-start(f32[256,128]{1,0:T(8,128)S(1)} %get-tuple-element.65.sent_even), channel_id=1, source_target_pairs={{0,4},{1,5},{2,6},{3,7},{4,0},{5,1},{6,2},{7,3},{8,12},{9,13},{10,... | collective-permute-start | bytes 393224 | tf_op jit(solution)/shard_map/ppermute | solution.py:80
  52.7 0.7 collective-permute-done.17.got_even
  53.4 0.2 collective-permute-start.12
  53.7 3.9 %collective-permute-start.21 = (f32[512,128]{1,0:T(8,128)S(1)}, f32[512,128]{1,0:T(8,128)S(1)}, u32[]{:S(2)}, u32[]{:S(2)}) collective-permute-start(f32[512,128]{1,0:T(8,128)S(1)} %shard_map.113.far_re), channel_id=1, source_target_pairs={{0,8},{1,2},{2,1},{3,11},{4,12},{5,6},{6,5},{7,15},{8,0},{9,10},{1... | collective-permute-start | bytes 786440 | tf_op jit(solution)/shard_map/ppermute | solution.py:80
  57.7 2.9 %collective-permute-done.9.got_even = f32[256,128]{1,0:T(8,128)S(1)} collective-permute-done((f32[256,128]{1,0:T(8,128)S(1)}, f32[256,128]{1,0:T(8,128)S(1)}, u32[]{:S(2)}, u32[]{:S(2)}) %collective-permute-start.9) | collective-permute-done | bytes 131104 | tf_op jit(solution)/shard_map/ppermute | solution.py:80
  60.6 1.9 %collective-permute-start.22 = (f32[512,128]{1,0:T(8,128)S(1)}, f32[512,128]{1,0:T(8,128)S(1)}, u32[]{:S(2)}, u32[]{:S(2)}) collective-permute-start(f32[512,128]{1,0:T(8,128)S(1)} %shard_map.115.far_im), channel_id=1, source_target_pairs={{0,8},{1,2},{2,1},{3,11},{4,12},{5,6},{6,5},{7,15},{8,0},{9,10},{1... | collective-permute-start | bytes 786440 | tf_op jit(solution)/shard_map/ppermute | solution.py:80
  62.7 0.5 collective-permute-start.20
  63.2 0.1 collective-permute-done.21.odd_re
  63.3 3.7 %collective-permute-done.22.odd_im = f32[512,128]{1,0:T(8,128)S(1)} collective-permute-done((f32[512,128]{1,0:T(8,128)S(1)}, f32[512,128]{1,0:T(8,128)S(1)}, u32[]{:S(2)}, u32[]{:S(2)}) %collective-permute-start.22) | collective-permute-done | bytes 262176 | tf_op jit(solution)/shard_map/ppermute | solution.py:80
  67.0 7.4 %shard_map.116 = (f32[2,4,512,128]{3,2,1,0:T(8,128)S(1)}, f32[2,512,128]{2,1,0:T(8,128)S(1)}, f32[2,512,128]{2,1,0:T(8,128)S(1)}, f32[2,2,256,128]{3,2,1,0:T(8,128)S(1)}, f32[2,2,256,128]{3,2,1,0:T(8,128)S(1)}) custom-call(s32[1,1,8]{2,1,0:T(1,128)S(1)} %get-tuple-element.46.order, s32[1,1,2,8]{3,2,1,0:T(2,128)S(1)} %get-tuple-element.47.offs, ...), custom_call_target="tpu_custom_call" | custom-call | tf_op jit(solution)/shard_map/pallas_call | solution.py:27
  74.5 1.9 %collective-permute-done.27.right = f32[1024,128]{1,0:T(8,128)S(1)} collective-permute-done((f32[1024,128]{1,0:T(8,128)S(1)}, f32[1024,128]{1,0:T(8,128)S(1)}, u32[]{:S(2)}, u32[]{:S(2)}) %collective-permute-start.27) | collective-permute-done | bytes 524320 | tf_op jit(solution)/shard_map/ppermute | solution.py:380
  76.5 14.3 %all_to_all.23 = f32[8,128,128]{2,1,0:T(8,128)S(1)} all-to-all(f32[8,128,128]{2,1,0:T(8,128)S(1)} %bitcast.9), channel_id=1, replica_groups={{0,2,4,6,8,10,12,14},{1,3,5,7,9,11,13,15},{16,18,20,22,24,26,28,30},{17..., dimensions={0} | all-to-all | bytes 1048576 | tf_op jit(solution)/shard_map/all_to_all | solution.py:390
  90.8 1.7 %collective-permute-start.28 = (f32[128,128]{1,0:T(8,128)S(1)}, f32[128,128]{1,0:T(8,128)S(1)}, u32[]{:S(2)}, u32[]{:S(2)}) collective-permute-start(f32[128,128]{1,0:T(8,128)S(1)} %shard_map.120.left), channel_id=1, source_target_pairs={{0,16},{1,17},{2,18},{3,19},{4,20},{5,21},{6,22},{7,23},{8,24},{9,... | collective-permute-start | bytes 196616 | tf_op jit(solution)/shard_map/ppermute | solution.py:380
  92.6 4.2 %collective-permute-done.28.right = f32[128,128]{1,0:T(8,128)S(1)} collective-permute-done((f32[128,128]{1,0:T(8,128)S(1)}, f32[128,128]{1,0:T(8,128)S(1)}, u32[]{:S(2)}, u32[]{:S(2)}) %collective-permute-start.28) | collective-permute-done | bytes 65568 | tf_op jit(solution)/shard_map/ppermute | solution.py:380
  96.8 0.8 shard_map.121
  97.6 3.5 %all-to-all-start.1 = ((f32[8,128,128]{2,1,0:T(8,128)}), f32[8,128,128]{2,1,0:T(8,128)S(1)}, u32[]{:S(2)}, u32[]{:S(2)}) async-start(f32[8,128,128]{2,1,0:T(8,128)} %bitcast.5), calls=%async_computation.1 | async-start | bytes 1048576 | tf_op jit(solution)/shard_map/all_to_all | solution.py:390
  101.2 1.9 %collective-permute-start.24 = (f32[2,512,128]{2,1,0:T(8,128)}, f32[2,512,128]{2,1,0:T(8,128)}, u32[]{:S(2)}, u32[]{:S(2)}) collective-permute-start(f32[2,512,128]{2,1,0:T(8,128)} %copy-done.2), channel_id=1, source_target_pairs={{0,4},{1,2},{2,1},{3,7},{4,0},{5,6},{6,5},{7,3},{8,12},{9,10},{10,... | collective-permute-start | bytes 1572872 | tf_op jit(solution)/shard_map/ppermute | solution.py:80
  103.0 5.8 %all-to-all-done.1 = f32[8,128,128]{2,1,0:T(8,128)S(1)} async-done(((f32[8,128,128]{2,1,0:T(8,128)}), f32[8,128,128]{2,1,0:T(8,128)S(1)}, u32[]{:S(2)}, u32[]{:S(2)}) %all-to-all-start.1) | async-done | bytes 524320 | tf_op jit(solution)/shard_map/all_to_all | solution.py:390
  108.8 4.5 %collective-permute-done.24.x_odd = f32[2,512,128]{2,1,0:T(8,128)} collective-permute-done((f32[2,512,128]{2,1,0:T(8,128)}, f32[2,512,128]{2,1,0:T(8,128)}, u32[]{:S(2)}, u32[]{:S(2)}) %collective-permute-start.24) | collective-permute-done | bytes 524320 | tf_op jit(solution)/shard_map/ppermute | solution.py:80
  113.3 1.6 %copy-done.1 = f32[2,4,512,128]{3,2,1,0:T(8,128)S(1)} copy-done((f32[2,4,512,128]{3,2,1,0:T(8,128)S(1)}, f32[2,4,512,128]{3,2,1,0:T(8,128)}, u32[]{:S(2)}) %copy-start.1) | copy-done | bytes 2097176
  114.9 1.2 shard_map.117
  116.1 1.4 %collective-permute-start.25 = (f32[2,2,128,128]{3,2,1,0:T(8,128)S(1)}, f32[2,2,128,128]{3,2,1,0:T(8,128)S(1)}, u32[]{:S(2)}, u32[]{:S(2)}) collective-permute-start(f32[2,2,128,128]{3,2,1,0:T(8,128)S(1)} %get-tuple-element.78), channel_id=1, source_target_pairs={{0,4},{1,5},{2,6},{3,7},{4,0},{5,1},{6,2},{7,3},{8,12},{9,13},{10,... | collective-permute-start | bytes 786440 | tf_op jit(solution)/shard_map/ppermute | solution.py:80
  117.5 0.7 collective-permute-start.26
  118.2 10.8 %collective-permute-done.25.y_even = f32[2,2,128,128]{3,2,1,0:T(8,128)S(1)} collective-permute-done((f32[2,2,128,128]{3,2,1,0:T(8,128)S(1)}, f32[2,2,128,128]{3,2,1,0:T(8,128)S(1)}, u32[]{:S(2)}, u32[]{:S(2)}) %collective-permute-start.25) | collective-permute-done | bytes 262176 | tf_op jit(solution)/shard_map/ppermute | solution.py:80
  128.9 0.9 shard_map.118
  129.8 1.1 shard_map.122
  (44 shorter events, 1.1 us)
Async XLA Ops:
  1.8 12.5 %collective-permute-start = (f32[2,128,128]{2,1,0:T(8,128)S(1)}, f32[2,128,128]{2,1,0:T(8,128)S(1)}, u32[]{:S(2)}, u32[]{:S(2)}) collective-permute-start(f32[2,128,128]{2,1,0:T(8,128)S(1)} %get-tuple-element.49), channel_id=1, source_target_pairs={{0,4},{1,5},{2,6},{3,7},{4,0},{5,1},{6,2},{7,3},{8,12},{9,13},{10,... | collective-permute-start | bytes 393224 | tf_op jit(solution)/shard_map/ppermute | solution.py:80
  4.8 11.5 %collective-permute-start.1 = (f32[2,128,128]{2,1,0:T(8,128)S(1)}, f32[2,128,128]{2,1,0:T(8,128)S(1)}, u32[]{:S(2)}, u32[]{:S(2)}) collective-permute-start(f32[2,128,128]{2,1,0:T(8,128)S(1)} %get-tuple-element.50), channel_id=1, source_target_pairs={{0,2},{1,3},{2,0},{3,1},{4,8},{5,9},{6,10},{7,11},{8,4},{9,5},{10,... | collective-permute-start | bytes 393224 | tf_op jit(solution)/shard_map/ppermute | solution.py:80
  6.3 10.1 %collective-permute-start.2 = (f32[2,128,128]{2,1,0:T(8,128)S(1)}, f32[2,128,128]{2,1,0:T(8,128)S(1)}, u32[]{:S(2)}, u32[]{:S(2)}) collective-permute-start(f32[2,128,128]{2,1,0:T(8,128)S(1)} %get-tuple-element.51), channel_id=1, source_target_pairs={{0,4},{1,5},{2,6},{3,7},{4,0},{5,1},{6,2},{7,3},{8,12},{9,13},{10,... | collective-permute-start | bytes 393224 | tf_op jit(solution)/shard_map/ppermute | solution.py:80
  7.9 8.6 %collective-permute-start.3 = (f32[2,128,128]{2,1,0:T(8,128)S(1)}, f32[2,128,128]{2,1,0:T(8,128)S(1)}, u32[]{:S(2)}, u32[]{:S(2)}) collective-permute-start(f32[2,128,128]{2,1,0:T(8,128)S(1)} %get-tuple-element.52), channel_id=1, source_target_pairs={{0,2},{1,3},{2,0},{3,1},{4,8},{5,9},{6,10},{7,11},{8,4},{9,5},{10,... | collective-permute-start | bytes 393224 | tf_op jit(solution)/shard_map/ppermute | solution.py:80
  10.7 10.8 %collective-permute-start.4 = (f32[2,256,128]{2,1,0:T(8,128)S(1)}, f32[2,256,128]{2,1,0:T(8,128)S(1)}, u32[]{:S(2)}, u32[]{:S(2)}) collective-permute-start(f32[2,256,128]{2,1,0:T(8,128)S(1)} %get-tuple-element.53), channel_id=1, source_target_pairs={{0,1},{1,0},{2,3},{3,2},{4,5},{5,4},{6,7},{7,6},{8,9},{9,8},{10,11... | collective-permute-start | bytes 786440 | tf_op jit(solution)/shard_map/ppermute | solution.py:80
  14.3 7.2 %collective-permute-start.5 = (f32[2,256,128]{2,1,0:T(8,128)S(1)}, f32[2,256,128]{2,1,0:T(8,128)S(1)}, u32[]{:S(2)}, u32[]{:S(2)}) collective-permute-start(f32[2,256,128]{2,1,0:T(8,128)S(1)} %get-tuple-element.54), channel_id=1, source_target_pairs={{0,8},{1,2},{2,1},{3,11},{4,12},{5,6},{6,5},{7,15},{8,0},{9,10},{1... | collective-permute-start | bytes 786440 | tf_op jit(solution)/shard_map/ppermute | solution.py:80
  16.4 5.2 %collective-permute-start.6 = (f32[2,2,128,128]{3,2,1,0:T(8,128)S(1)}, f32[2,2,128,128]{3,2,1,0:T(8,128)S(1)}, u32[]{:S(2)}, u32[]{:S(2)}) collective-permute-start(f32[2,2,128,128]{3,2,1,0:T(8,128)S(1)} %shard_map.105), channel_id=1, source_target_pairs={{0,1},{1,0},{2,3},{3,2},{4,5},{5,4},{6,7},{7,6},{8,9},{9,8},{10,11... | collective-permute-start | bytes 786440 | tf_op jit(solution)/shard_map/ppermute | solution.py:80
  16.5 7.0 %collective-permute-start.7 = (f32[2,2,128,128]{3,2,1,0:T(8,128)S(1)}, f32[2,2,128,128]{3,2,1,0:T(8,128)S(1)}, u32[]{:S(2)}, u32[]{:S(2)}) collective-permute-start(f32[2,2,128,128]{3,2,1,0:T(8,128)S(1)} %shard_map.106), channel_id=1, source_target_pairs={{0,8},{1,2},{2,1},{3,11},{4,12},{5,6},{6,5},{7,15},{8,0},{9,10},{1... | collective-permute-start | bytes 786440 | tf_op jit(solution)/shard_map/ppermute | solution.py:80
  30.7 12.7 %collective-permute-start.8 = (f32[2,512,128]{2,1,0:T(8,128)S(1)}, f32[2,512,128]{2,1,0:T(8,128)S(1)}, u32[]{:S(2)}, u32[]{:S(2)}) collective-permute-start(f32[2,512,128]{2,1,0:T(8,128)S(1)} %get-tuple-element.61), channel_id=1, source_target_pairs={{0,1},{1,0},{2,3},{3,2},{4,5},{5,4},{6,7},{7,6},{8,9},{9,8},{10,11... | collective-permute-start | bytes 1572872 | tf_op jit(solution)/shard_map/ppermute | solution.py:80
  30.7 6.5 %collective-permute-start.13 = (f32[512,128]{1,0:T(8,128)S(1)}, f32[512,128]{1,0:T(8,128)S(1)}, u32[]{:S(2)}, u32[]{:S(2)}) collective-permute-start(f32[512,128]{1,0:T(8,128)S(1)} %get-tuple-element.67), channel_id=1, source_target_pairs={{0,8},{1,2},{2,1},{3,11},{4,12},{5,6},{6,5},{7,15},{8,0},{9,10},{1... | collective-permute-start | bytes 786440 | tf_op jit(solution)/shard_map/ppermute | solution.py:80
  32.9 7.2 %collective-permute-start.16 = (f32[512,128]{1,0:T(8,128)S(1)}, f32[512,128]{1,0:T(8,128)S(1)}, u32[]{:S(2)}, u32[]{:S(2)}) collective-permute-start(f32[512,128]{1,0:T(8,128)S(1)} %get-tuple-element.70), channel_id=1, source_target_pairs={{0,8},{1,2},{2,1},{3,11},{4,12},{5,6},{6,5},{7,15},{8,0},{9,10},{1... | collective-permute-start | bytes 786440 | tf_op jit(solution)/shard_map/ppermute | solution.py:80
  37.3 12.1 %collective-permute-start.14 = (f32[256,128]{1,0:T(8,128)S(1)}, f32[256,128]{1,0:T(8,128)S(1)}, u32[]{:S(2)}, u32[]{:S(2)}) collective-permute-start(f32[256,128]{1,0:T(8,128)S(1)} %get-tuple-element.68.sent_even), channel_id=1, source_target_pairs={{0,4},{1,5},{2,6},{3,7},{4,0},{5,1},{6,2},{7,3},{8,12},{9,13},{10,... | collective-permute-start | bytes 393224 | tf_op jit(solution)/shard_map/ppermute | solution.py:80
  39.8 9.8 %collective-permute-start.15 = (f32[256,128]{1,0:T(8,128)S(1)}, f32[256,128]{1,0:T(8,128)S(1)}, u32[]{:S(2)}, u32[]{:S(2)}) collective-permute-start(f32[256,128]{1,0:T(8,128)S(1)} %get-tuple-element.69.sent_odd), channel_id=1, source_target_pairs={{0,2},{1,3},{2,0},{3,1},{4,8},{5,9},{6,10},{7,11},{8,4},{9,5},{10,... | collective-permute-start | bytes 393224 | tf_op jit(solution)/shard_map/ppermute | solution.py:80
  40.1 13.3 %collective-permute-start.17 = (f32[256,128]{1,0:T(8,128)S(1)}, f32[256,128]{1,0:T(8,128)S(1)}, u32[]{:S(2)}, u32[]{:S(2)}) collective-permute-start(f32[256,128]{1,0:T(8,128)S(1)} %get-tuple-element.71.sent_even), channel_id=1, source_target_pairs={{0,4},{1,5},{2,6},{3,7},{4,0},{5,1},{6,2},{7,3},{8,12},{9,13},{10,... | collective-permute-start | bytes 393224 | tf_op jit(solution)/shard_map/ppermute | solution.py:80
  43.0 10.7 %collective-permute-start.18 = (f32[256,128]{1,0:T(8,128)S(1)}, f32[256,128]{1,0:T(8,128)S(1)}, u32[]{:S(2)}, u32[]{:S(2)}) collective-permute-start(f32[256,128]{1,0:T(8,128)S(1)} %get-tuple-element.72.sent_odd), channel_id=1, source_target_pairs={{0,2},{1,3},{2,0},{3,1},{4,8},{5,9},{6,10},{7,11},{8,4},{9,5},{10,... | collective-permute-start | bytes 393224 | tf_op jit(solution)/shard_map/ppermute | solution.py:80
  43.4 17.1 %collective-permute-start.9 = (f32[256,128]{1,0:T(8,128)S(1)}, f32[256,128]{1,0:T(8,128)S(1)}, u32[]{:S(2)}, u32[]{:S(2)}) collective-permute-start(f32[256,128]{1,0:T(8,128)S(1)} %get-tuple-element.62.sent_even), channel_id=1, source_target_pairs={{0,4},{1,5},{2,6},{3,7},{4,0},{5,1},{6,2},{7,3},{8,12},{9,13},{10,... | collective-permute-start | bytes 393224 | tf_op jit(solution)/shard_map/ppermute | solution.py:80
  49.3 13.1 %collective-permute-start.10 = (f32[256,128]{1,0:T(8,128)S(1)}, f32[256,128]{1,0:T(8,128)S(1)}, u32[]{:S(2)}, u32[]{:S(2)}) collective-permute-start(f32[256,128]{1,0:T(8,128)S(1)} %get-tuple-element.63.sent_odd), channel_id=1, source_target_pairs={{0,2},{1,3},{2,0},{3,1},{4,8},{5,9},{6,10},{7,11},{8,4},{9,5},{10,... | collective-permute-start | bytes 393224 | tf_op jit(solution)/shard_map/ppermute | solution.py:80
  49.6 13.0 %collective-permute-start.11 = (f32[256,128]{1,0:T(8,128)S(1)}, f32[256,128]{1,0:T(8,128)S(1)}, u32[]{:S(2)}, u32[]{:S(2)}) collective-permute-start(f32[256,128]{1,0:T(8,128)S(1)} %get-tuple-element.65.sent_even), channel_id=1, source_target_pairs={{0,4},{1,5},{2,6},{3,7},{4,0},{5,1},{6,2},{7,3},{8,12},{9,13},{10,... | collective-permute-start | bytes 393224 | tf_op jit(solution)/shard_map/ppermute | solution.py:80
  53.4 9.2 %collective-permute-start.12 = (f32[256,128]{1,0:T(8,128)S(1)}, f32[256,128]{1,0:T(8,128)S(1)}, u32[]{:S(2)}, u32[]{:S(2)}) collective-permute-start(f32[256,128]{1,0:T(8,128)S(1)} %get-tuple-element.66.sent_odd), channel_id=1, source_target_pairs={{0,2},{1,3},{2,0},{3,1},{4,8},{5,9},{6,10},{7,11},{8,4},{9,5},{10,... | collective-permute-start | bytes 393224 | tf_op jit(solution)/shard_map/ppermute | solution.py:80
  53.7 9.6 %collective-permute-start.21 = (f32[512,128]{1,0:T(8,128)S(1)}, f32[512,128]{1,0:T(8,128)S(1)}, u32[]{:S(2)}, u32[]{:S(2)}) collective-permute-start(f32[512,128]{1,0:T(8,128)S(1)} %shard_map.113.far_re), channel_id=1, source_target_pairs={{0,8},{1,2},{2,1},{3,11},{4,12},{5,6},{6,5},{7,15},{8,0},{9,10},{1... | collective-permute-start | bytes 786440 | tf_op jit(solution)/shard_map/ppermute | solution.py:80
  60.6 6.4 %collective-permute-start.22 = (f32[512,128]{1,0:T(8,128)S(1)}, f32[512,128]{1,0:T(8,128)S(1)}, u32[]{:S(2)}, u32[]{:S(2)}) collective-permute-start(f32[512,128]{1,0:T(8,128)S(1)} %shard_map.115.far_im), channel_id=1, source_target_pairs={{0,8},{1,2},{2,1},{3,11},{4,12},{5,6},{6,5},{7,15},{8,0},{9,10},{1... | collective-permute-start | bytes 786440 | tf_op jit(solution)/shard_map/ppermute | solution.py:80
  62.5 4.5 %collective-permute-start.19 = (f32[512,128]{1,0:T(8,128)S(1)}, f32[512,128]{1,0:T(8,128)S(1)}, u32[]{:S(2)}, u32[]{:S(2)}) collective-permute-start(f32[512,128]{1,0:T(8,128)S(1)} %shard_map.109.near_re), channel_id=1, source_target_pairs={{0,1},{1,0},{2,3},{3,2},{4,5},{5,4},{6,7},{7,6},{8,9},{9,8},{10,11... | collective-permute-start | bytes 786440 | tf_op jit(solution)/shard_map/ppermute | solution.py:80
  62.7 4.3 %collective-permute-start.20 = (f32[512,128]{1,0:T(8,128)S(1)}, f32[512,128]{1,0:T(8,128)S(1)}, u32[]{:S(2)}, u32[]{:S(2)}) collective-permute-start(f32[512,128]{1,0:T(8,128)S(1)} %shard_map.111.near_im), channel_id=1, source_target_pairs={{0,1},{1,0},{2,3},{3,2},{4,5},{5,4},{6,7},{7,6},{8,9},{9,8},{10,11... | collective-permute-start | bytes 786440 | tf_op jit(solution)/shard_map/ppermute | solution.py:80
  74.4 16.4 %copy-start = (f32[2,4,512,128]{3,2,1,0:T(8,128)}, f32[2,4,512,128]{3,2,1,0:T(8,128)S(1)}, u32[]{:S(2)}) copy-start(f32[2,4,512,128]{3,2,1,0:T(8,128)S(1)} %get-tuple-element.74.accum) | copy-start | bytes 6291460
  74.4 23.2 %copy-start.2 = (f32[2,512,128]{2,1,0:T(8,128)}, f32[2,512,128]{2,1,0:T(8,128)S(1)}, u32[]{:S(2)}) copy-start(f32[2,512,128]{2,1,0:T(8,128)S(1)} %get-tuple-element.76) | copy-start | bytes 1572868
  74.4 23.2 %copy-start.3 = (f32[2,512,128]{2,1,0:T(8,128)}, f32[2,512,128]{2,1,0:T(8,128)S(1)}, u32[]{:S(2)}) copy-start(f32[2,512,128]{2,1,0:T(8,128)S(1)} %get-tuple-element.75) | copy-start | bytes 1572868
  74.4 2.0 %collective-permute-start.27 = (f32[1024,128]{1,0:T(8,128)S(1)}, f32[1024,128]{1,0:T(8,128)S(1)}, u32[]{:S(2)}, u32[]{:S(2)}) collective-permute-start(f32[1024,128]{1,0:T(8,128)S(1)} %bitcast.15), channel_id=1, source_target_pairs={{0,1},{1,0},{2,3},{3,2},{4,5},{5,4},{6,7},{7,6},{8,9},{9,8},{10,11... | collective-permute-start | bytes 1572872 | tf_op jit(solution)/shard_map/ppermute | solution.py:380
  90.8 5.9 %collective-permute-start.28 = (f32[128,128]{1,0:T(8,128)S(1)}, f32[128,128]{1,0:T(8,128)S(1)}, u32[]{:S(2)}, u32[]{:S(2)}) collective-permute-start(f32[128,128]{1,0:T(8,128)S(1)} %shard_map.120.left), channel_id=1, source_target_pairs={{0,16},{1,17},{2,18},{3,19},{4,20},{5,21},{6,22},{7,23},{8,24},{9,... | collective-permute-start | bytes 196616 | tf_op jit(solution)/shard_map/ppermute | solution.py:380
  97.6 11.2 %all-to-all-start.1 = ((f32[8,128,128]{2,1,0:T(8,128)}), f32[8,128,128]{2,1,0:T(8,128)S(1)}, u32[]{:S(2)}, u32[]{:S(2)}) async-start(f32[8,128,128]{2,1,0:T(8,128)} %bitcast.5), calls=%async_computation.1 | async-start | bytes 1048576 | tf_op jit(solution)/shard_map/all_to_all | solution.py:390
  101.1 7.7 %collective-permute-start.23 = (f32[2,512,128]{2,1,0:T(8,128)}, f32[2,512,128]{2,1,0:T(8,128)S(1)}, u32[]{:S(2)}, u32[]{:S(2)}) collective-permute-start(f32[2,512,128]{2,1,0:T(8,128)} %copy-done.3), channel_id=1, source_target_pairs={{0,1},{1,0},{2,3},{3,2},{4,5},{5,4},{6,7},{7,6},{8,9},{9,8},{10,11... | collective-permute-start | bytes 1572872 | tf_op jit(solution)/shard_map/ppermute | solution.py:80
  101.2 12.1 %collective-permute-start.24 = (f32[2,512,128]{2,1,0:T(8,128)}, f32[2,512,128]{2,1,0:T(8,128)}, u32[]{:S(2)}, u32[]{:S(2)}) collective-permute-start(f32[2,512,128]{2,1,0:T(8,128)} %copy-done.2), channel_id=1, source_target_pairs={{0,4},{1,2},{2,1},{3,7},{4,0},{5,6},{6,5},{7,3},{8,12},{9,10},{10,... | collective-permute-start | bytes 1572872 | tf_op jit(solution)/shard_map/ppermute | solution.py:80
  108.8 21.0 %collective-permute-start.29 = (f32[1024,128]{1,0:T(8,128)S(1)}, f32[1024,128]{1,0:T(8,128)S(1)}, u32[]{:S(2)}, u32[]{:S(2)}) collective-permute-start(f32[1024,128]{1,0:T(8,128)S(1)} %bitcast.11), channel_id=1, source_target_pairs={{0,1},{1,0},{2,3},{3,2},{4,5},{5,4},{6,7},{7,6},{8,9},{9,8},{10,11... | collective-permute-start | bytes 1572872 | tf_op jit(solution)/shard_map/ppermute | solution.py:380
  113.3 1.6 %copy-start.1 = (f32[2,4,512,128]{3,2,1,0:T(8,128)S(1)}, f32[2,4,512,128]{3,2,1,0:T(8,128)}, u32[]{:S(2)}) copy-start(f32[2,4,512,128]{3,2,1,0:T(8,128)} %copy-done) | copy-start | bytes 6291460
  116.1 12.9 %collective-permute-start.25 = (f32[2,2,128,128]{3,2,1,0:T(8,128)S(1)}, f32[2,2,128,128]{3,2,1,0:T(8,128)S(1)}, u32[]{:S(2)}, u32[]{:S(2)}) collective-permute-start(f32[2,2,128,128]{3,2,1,0:T(8,128)S(1)} %get-tuple-element.78), channel_id=1, source_target_pairs={{0,4},{1,5},{2,6},{3,7},{4,0},{5,1},{6,2},{7,3},{8,12},{9,13},{10,... | collective-permute-start | bytes 786440 | tf_op jit(solution)/shard_map/ppermute | solution.py:80
  117.5 11.5 %collective-permute-start.26 = (f32[2,2,128,128]{3,2,1,0:T(8,128)S(1)}, f32[2,2,128,128]{3,2,1,0:T(8,128)S(1)}, u32[]{:S(2)}, u32[]{:S(2)}) collective-permute-start(f32[2,2,128,128]{3,2,1,0:T(8,128)S(1)} %get-tuple-element.79), channel_id=1, source_target_pairs={{0,2},{1,3},{2,0},{3,1},{4,8},{5,9},{6,10},{7,11},{8,4},{9,5},{10,... | collective-permute-start | bytes 786440 | tf_op jit(solution)/shard_map/ppermute | solution.py:80

commit v2 on v1

--- a/solution.py
+++ b/solution.py
@@ -19,7 +19,7 @@
 HBM = pl.BlockSpec(memory_space=pltpu.HBM)
 
 
-def call(kernel, out_shape, operands, in_specs=None, scratch=(), room=0):
+def call(kernel, out_shape, operands, in_specs=None, scratch=(), room=0, out_spec=VMEM):
     outs = jax.tree.leaves(out_shape)
     specs = in_specs or [VMEM] * len(operands)
     held = [a for a, spec in zip(operands, specs) if spec is VMEM]
@@ -28,7 +28,7 @@
         kernel,
         out_shape=out_shape,
         in_specs=specs,
-        out_specs=jax.tree.map(lambda _: VMEM, out_shape),
+        out_specs=jax.tree.map(lambda _: out_spec, out_shape),
         scratch_shapes=scratch,
         compiler_params=pltpu.CompilerParams(vmem_limit_bytes=need + (1 << 20)),
     )(*operands)
@@ -406,15 +406,20 @@
         out[at : at + size, :] = total
 
 
-def finish_probe_kernel(rate, keep, got, probe_re, probe_im, out_re, out_im):
+def finish_probe_kernel(rate, keep, got, probe_re, probe_im, out_re, out_im, done, sems):
     px = parity(SX)
-    f = probe_re.shape[1]
-    h = f // 2
-    for mode, part in ((px, keep), (1 - px, got)):
+    h = probe_re.shape[1] // 2
+    copies = []
+    for at, (mode, part) in enumerate(((px, keep), (1 - px, got))):
         for c, (probe, out) in enumerate(((probe_re, out_re), (probe_im, out_im))):
+            spot = 2 * at + c
             for lb in range(2):
                 cols = slice(lb * h, (lb + 1) * h)
-                out[mode, :, cols] = probe[mode, :, cols] + rate * part[c, lb]
+                done[spot, :, cols] = probe[mode, :, cols] + rate * part[c, lb]
+            copies.append(pltpu.make_async_copy(done.at[spot], out.at[mode], sems.at[spot]))
+            copies[spot].start()
+    for copy in copies:
+        copy.wait()
 
 
 def local(object_re, object_im, probe_re, probe_im, amplitudes, offsets, visit_order):
@@ -512,6 +517,8 @@
         functools.partial(finish_probe_kernel, probe_rate),
         [f32(2, f, f)] * 2,
         (total.reshape(piece), got.reshape(piece), *probe),
+        scratch=[pltpu.VMEM((4, f, f), jnp.float32), pltpu.SemaphoreType.DMA((4,))],
+        out_spec=HBM,
     )
     return (out_re, out_im, probe_out[0], probe_out[1])
 

time: 131 us -> 131 us (level)
  no operation moved by 1% of the time
where the time goes in v2:
time: 131 us
  waiting for transfers between devices  47.4 us (36%)
  starting transfers between devices  42.2 us (32%)
  Pallas kernels  24.4 us (19%)
  blocking collectives  14.3 us (11%)
  local copies, waits for them, and re-layouts  1.61 us (1%)
    ppermute x27, starting transfers between devices, pair_exchange(): return lax.ppermute(block, (SY, SX), perm)  36.9 us
    ppermute x27, waiting for transfers between devices, pair_exchange(): return lax.ppermute(block, (SY, SX), perm)  35.6 us
    pallas_call x21, Pallas kernels, call(): pl.pallas_call(kernel, out_shape=out_shape, in_specs=specs, out_specs=jax...  24.4 us
    all_to_all x1, blocking collectives, block_exchange(): lax.all_to_all(pieces, (SY, SX), 0, 0, tiled=True, axis_index_groups=list...  14.3 us
    ppermute x3, waiting for transfers between devices, flip_exchange(): return lax.ppermute(block, (SY, SX), perm)  6.09 us
    all_to_all x1, waiting for transfers between devices, block_exchange(): lax.all_to_all(pieces, (SY, SX), 0, 0, tiled=True, axis_index_groups=list...  5.78 us
    all_to_all x1, starting transfers between devices, block_exchange(): lax.all_to_all(pieces, (SY, SX), 0, 0, tiled=True, axis_index_groups=list...  3.49 us
  transfers between devices with their start and end apart: 31, of which 13 were waited for; matrix products, arithmetic and copies ran while one was open for 0% of the time, Pallas kernels for 5%

profile of v2, /device:TPU:0, one launch (start us, length us, event | category | flops | bytes accessed | tf_op | source)
XLA Modules:
  0.0 131.0 jit_solution(15753716864735526718)
XLA Ops:
  0.6 1.1 shard_map.104
  1.8 3.1 %collective-permute-start = (f32[2,128,128]{2,1,0:T(8,128)S(1)}, f32[2,128,128]{2,1,0:T(8,128)S(1)}, u32[]{:S(2)}, u32[]{:S(2)}) collective-permute-start(f32[2,128,128]{2,1,0:T(8,128)S(1)} %get-tuple-element.49), channel_id=1, source_target_pairs={{0,4},{1,5},{2,6},{3,7},{4,0},{5,1},{6,2},{7,3},{8,12},{9,13},{10,... | collective-permute-start | bytes 393224 | tf_op jit(solution)/shard_map/ppermute | solution.py:80
  4.8 1.5 %collective-permute-start.1 = (f32[2,128,128]{2,1,0:T(8,128)S(1)}, f32[2,128,128]{2,1,0:T(8,128)S(1)}, u32[]{:S(2)}, u32[]{:S(2)}) collective-permute-start(f32[2,128,128]{2,1,0:T(8,128)S(1)} %get-tuple-element.50), channel_id=1, source_target_pairs={{0,2},{1,3},{2,0},{3,1},{4,8},{5,9},{6,10},{7,11},{8,4},{9,5},{10,... | collective-permute-start | bytes 393224 | tf_op jit(solution)/shard_map/ppermute | solution.py:80
  6.3 1.5 %collective-permute-start.2 = (f32[2,128,128]{2,1,0:T(8,128)S(1)}, f32[2,128,128]{2,1,0:T(8,128)S(1)}, u32[]{:S(2)}, u32[]{:S(2)}) collective-permute-start(f32[2,128,128]{2,1,0:T(8,128)S(1)} %get-tuple-element.51), channel_id=1, source_target_pairs={{0,4},{1,5},{2,6},{3,7},{4,0},{5,1},{6,2},{7,3},{8,12},{9,13},{10,... | collective-permute-start | bytes 393224 | tf_op jit(solution)/shard_map/ppermute | solution.py:80
  7.9 1.5 %collective-permute-start.3 = (f32[2,128,128]{2,1,0:T(8,128)S(1)}, f32[2,128,128]{2,1,0:T(8,128)S(1)}, u32[]{:S(2)}, u32[]{:S(2)}) collective-permute-start(f32[2,128,128]{2,1,0:T(8,128)S(1)} %get-tuple-element.52), channel_id=1, source_target_pairs={{0,2},{1,3},{2,0},{3,1},{4,8},{5,9},{6,10},{7,11},{8,4},{9,5},{10,... | collective-permute-start | bytes 393224 | tf_op jit(solution)/shard_map/ppermute | solution.py:80
  9.4 1.3 %shard_map.103 = (f32[2,256,128]{2,1,0:T(8,128)S(1)}, f32[2,256,128]{2,1,0:T(8,128)S(1)}, f32[2,2,256,128]{3,2,1,0:T(8,128)S(1)}) custom-call(f32[256,256]{1,0:T(8,128)} %obj_re.3, f32[256,256]{1,0:T(8,128)} %obj_im.3), custom_call_target="tpu_custom_call" | custom-call | tf_op jit(solution)/shard_map/pallas_call | solution.py:27
  10.8 3.5 %collective-permute-done.up_even.up_00 = f32[2,128,128]{2,1,0:T(8,128)S(1)} collective-permute-done((f32[2,128,128]{2,1,0:T(8,128)S(1)}, f32[2,128,128]{2,1,0:T(8,128)S(1)}, u32[]{:S(2)}, u32[]{:S(2)}) %collective-permute-start) | collective-permute-done | bytes 131104 | tf_op jit(solution)/shard_map/ppermute | solution.py:80
  14.3 2.0 %collective-permute-start.5 = (f32[2,256,128]{2,1,0:T(8,128)S(1)}, f32[2,256,128]{2,1,0:T(8,128)S(1)}, u32[]{:S(2)}, u32[]{:S(2)}) collective-permute-start(f32[2,256,128]{2,1,0:T(8,128)S(1)} %get-tuple-element.54), channel_id=1, source_target_pairs={{0,8},{1,2},{2,1},{3,11},{4,12},{5,6},{6,5},{7,15},{8,0},{9,10},{1... | collective-permute-start | bytes 786440 | tf_op jit(solution)/shard_map/ppermute | solution.py:80
  16.5 2.1 %collective-permute-start.7 = (f32[2,2,128,128]{3,2,1,0:T(8,128)S(1)}, f32[2,2,128,128]{3,2,1,0:T(8,128)S(1)}, u32[]{:S(2)}, u32[]{:S(2)}) collective-permute-start(f32[2,2,128,128]{3,2,1,0:T(8,128)S(1)} %shard_map.106), channel_id=1, source_target_pairs={{0,8},{1,2},{2,1},{3,11},{4,12},{5,6},{6,5},{7,15},{8,0},{9,10},{1... | collective-permute-start | bytes 786440 | tf_op jit(solution)/shard_map/ppermute | solution.py:80
  18.7 2.8 %shard_map.102 = (bf16[512,512]{1,0:T(8,128)(2,1)S(1)}, bf16[512,512]{1,0:T(8,128)(2,1)S(1)}, f32[8,128]{1,0:T(8,128)S(1)}, s32[1,1,8]{2,1,0:T(1,128)S(1)}, s32[...) custom-call(s32[1,1,8]{2,1,0:T(1,128)} %order_hbm.1, ...), custom_call_target="tpu_custom_call" | custom-call | tf_op jit(solution)/shard_map/pallas_call | solution.py:27
  21.6 2.0 %collective-permute-done.7.c_odd = f32[2,2,128,128]{3,2,1,0:T(8,128)S(1)} collective-permute-done((f32[2,2,128,128]{3,2,1,0:T(8,128)S(1)}, f32[2,2,128,128]{3,2,1,0:T(8,128)S(1)}, u32[]{:S(2)}, u32[]{:S(2)}) %collective-permute-start.7) | collective-permute-done | bytes 262176 | tf_op jit(solution)/shard_map/ppermute | solution.py:80
  23.5 7.1 %shard_map.107 = (f32[2,4,512,128]{3,2,1,0:T(8,128)S(1)}, f32[2,4,512,128]{3,2,1,0:T(8,128)S(1)}, f32[2,512,128]{2,1,0:T(8,128)S(1)}, f32[512,128]{1,0:T(8,128)S...) custom-call(s32[1,1,8]{2,1,0:T(1,128)S(1)} %get-tuple-element.46.order, ...), custom_call_target="tpu_custom_call" | custom-call | tf_op jit(solution)/shard_map/pallas_call | solution.py:27
  30.7 2.1 %collective-permute-start.13 = (f32[512,128]{1,0:T(8,128)S(1)}, f32[512,128]{1,0:T(8,128)S(1)}, u32[]{:S(2)}, u32[]{:S(2)}) collective-permute-start(f32[512,128]{1,0:T(8,128)S(1)} %get-tuple-element.67), channel_id=1, source_target_pairs={{0,8},{1,2},{2,1},{3,11},{4,12},{5,6},{6,5},{7,15},{8,0},{9,10},{1... | collective-permute-start | bytes 786440 | tf_op jit(solution)/shard_map/ppermute | solution.py:80
  32.9 0.1 collective-permute-start.16
  33.0 4.3 %collective-permute-done.13.x_got = f32[512,128]{1,0:T(8,128)S(1)} collective-permute-done((f32[512,128]{1,0:T(8,128)S(1)}, f32[512,128]{1,0:T(8,128)S(1)}, u32[]{:S(2)}, u32[]{:S(2)}) %collective-permute-start.13) | collective-permute-done | bytes 262176 | tf_op jit(solution)/shard_map/ppermute | solution.py:80
  37.3 2.6 %collective-permute-start.14 = (f32[256,128]{1,0:T(8,128)S(1)}, f32[256,128]{1,0:T(8,128)S(1)}, u32[]{:S(2)}, u32[]{:S(2)}) collective-permute-start(f32[256,128]{1,0:T(8,128)S(1)} %get-tuple-element.68.sent_even), channel_id=1, source_target_pairs={{0,4},{1,5},{2,6},{3,7},{4,0},{5,1},{6,2},{7,3},{8,12},{9,13},{10,... | collective-permute-start | bytes 393224 | tf_op jit(solution)/shard_map/ppermute | solution.py:80
  39.8 0.2 collective-permute-start.15
  40.1 2.9 %collective-permute-start.17 = (f32[256,128]{1,0:T(8,128)S(1)}, f32[256,128]{1,0:T(8,128)S(1)}, u32[]{:S(2)}, u32[]{:S(2)}) collective-permute-start(f32[256,128]{1,0:T(8,128)S(1)} %get-tuple-element.71.sent_even), channel_id=1, source_target_pairs={{0,4},{1,5},{2,6},{3,7},{4,0},{5,1},{6,2},{7,3},{8,12},{9,13},{10,... | collective-permute-start | bytes 393224 | tf_op jit(solution)/shard_map/ppermute | solution.py:80
  43.0 0.4 collective-permute-start.18
  43.4 2.7 %collective-permute-start.9 = (f32[256,128]{1,0:T(8,128)S(1)}, f32[256,128]{1,0:T(8,128)S(1)}, u32[]{:S(2)}, u32[]{:S(2)}) collective-permute-start(f32[256,128]{1,0:T(8,128)S(1)} %get-tuple-element.62.sent_even), channel_id=1, source_target_pairs={{0,4},{1,5},{2,6},{3,7},{4,0},{5,1},{6,2},{7,3},{8,12},{9,13},{10,... | collective-permute-start | bytes 393224 | tf_op jit(solution)/shard_map/ppermute | solution.py:80
  46.2 3.1 %collective-permute-done.14.got_even = f32[256,128]{1,0:T(8,128)S(1)} collective-permute-done((f32[256,128]{1,0:T(8,128)S(1)}, f32[256,128]{1,0:T(8,128)S(1)}, u32[]{:S(2)}, u32[]{:S(2)}) %collective-permute-start.14) | collective-permute-done | bytes 131104 | tf_op jit(solution)/shard_map/ppermute | solution.py:80
  49.3 0.2 collective-permute-start.10
  49.6 3.1 %collective-permute-start.11 = (f32[256,128]{1,0:T(8,128)S(1)}, f32[256,128]{1,0:T(8,128)S(1)}, u32[]{:S(2)}, u32[]{:S(2)}) collective-permute-start(f32[256,128]{1,0:T(8,128)S(1)} %get-tuple-element.65.sent_even), channel_id=1, source_target_pairs={{0,4},{1,5},{2,6},{3,7},{4,0},{5,1},{6,2},{7,3},{8,12},{9,13},{10,... | collective-permute-start | bytes 393224 | tf_op jit(solution)/shard_map/ppermute | solution.py:80
  52.7 0.7 collective-permute-done.17.got_even
  53.4 0.2 collective-permute-start.12
  53.7 3.9 %collective-permute-start.21 = (f32[512,128]{1,0:T(8,128)S(1)}, f32[512,128]{1,0:T(8,128)S(1)}, u32[]{:S(2)}, u32[]{:S(2)}) collective-permute-start(f32[512,128]{1,0:T(8,128)S(1)} %shard_map.113.far_re), channel_id=1, source_target_pairs={{0,8},{1,2},{2,1},{3,11},{4,12},{5,6},{6,5},{7,15},{8,0},{9,10},{1... | collective-permute-start | bytes 786440 | tf_op jit(solution)/shard_map/ppermute | solution.py:80
  57.7 2.9 %collective-permute-done.9.got_even = f32[256,128]{1,0:T(8,128)S(1)} collective-permute-done((f32[256,128]{1,0:T(8,128)S(1)}, f32[256,128]{1,0:T(8,128)S(1)}, u32[]{:S(2)}, u32[]{:S(2)}) %collective-permute-start.9) | collective-permute-done | bytes 131104 | tf_op jit(solution)/shard_map/ppermute | solution.py:80
  60.6 1.9 %collective-permute-start.22 = (f32[512,128]{1,0:T(8,128)S(1)}, f32[512,128]{1,0:T(8,128)S(1)}, u32[]{:S(2)}, u32[]{:S(2)}) collective-permute-start(f32[512,128]{1,0:T(8,128)S(1)} %shard_map.115.far_im), channel_id=1, source_target_pairs={{0,8},{1,2},{2,1},{3,11},{4,12},{5,6},{6,5},{7,15},{8,0},{9,10},{1... | collective-permute-start | bytes 786440 | tf_op jit(solution)/shard_map/ppermute | solution.py:80
  62.7 0.5 collective-permute-start.20
  63.2 0.1 collective-permute-done.21.odd_re
  63.3 3.7 %collective-permute-done.22.odd_im = f32[512,128]{1,0:T(8,128)S(1)} collective-permute-done((f32[512,128]{1,0:T(8,128)S(1)}, f32[512,128]{1,0:T(8,128)S(1)}, u32[]{:S(2)}, u32[]{:S(2)}) %collective-permute-start.22) | collective-permute-done | bytes 262176 | tf_op jit(solution)/shard_map/ppermute | solution.py:80
  67.0 7.4 %shard_map.116 = (f32[2,4,512,128]{3,2,1,0:T(8,128)S(1)}, f32[2,512,128]{2,1,0:T(8,128)S(1)}, f32[2,512,128]{2,1,0:T(8,128)S(1)}, f32[2,2,256,128]{3,2,1,0:T(8,128)S(1)}, f32[2,2,256,128]{3,2,1,0:T(8,128)S(1)}) custom-call(s32[1,1,8]{2,1,0:T(1,128)S(1)} %get-tuple-element.46.order, s32[1,1,2,8]{3,2,1,0:T(2,128)S(1)} %get-tuple-element.47.offs, ...), custom_call_target="tpu_custom_call" | custom-call | tf_op jit(solution)/shard_map/pallas_call | solution.py:27
  74.5 1.9 %collective-permute-done.27.right = f32[1024,128]{1,0:T(8,128)S(1)} collective-permute-done((f32[1024,128]{1,0:T(8,128)S(1)}, f32[1024,128]{1,0:T(8,128)S(1)}, u32[]{:S(2)}, u32[]{:S(2)}) %collective-permute-start.27) | collective-permute-done | bytes 524320 | tf_op jit(solution)/shard_map/ppermute | solution.py:380
  76.5 14.3 %all_to_all.23 = f32[8,128,128]{2,1,0:T(8,128)S(1)} all-to-all(f32[8,128,128]{2,1,0:T(8,128)S(1)} %bitcast.9), channel_id=1, replica_groups={{0,2,4,6,8,10,12,14},{1,3,5,7,9,11,13,15},{16,18,20,22,24,26,28,30},{17..., dimensions={0} | all-to-all | bytes 1048576 | tf_op jit(solution)/shard_map/all_to_all | solution.py:390
  90.8 1.7 %collective-permute-start.28 = (f32[128,128]{1,0:T(8,128)S(1)}, f32[128,128]{1,0:T(8,128)S(1)}, u32[]{:S(2)}, u32[]{:S(2)}) collective-permute-start(f32[128,128]{1,0:T(8,128)S(1)} %shard_map.120.left), channel_id=1, source_target_pairs={{0,16},{1,17},{2,18},{3,19},{4,20},{5,21},{6,22},{7,23},{8,24},{9,... | collective-permute-start | bytes 196616 | tf_op jit(solution)/shard_map/ppermute | solution.py:380
  92.6 4.2 %collective-permute-done.28.right = f32[128,128]{1,0:T(8,128)S(1)} collective-permute-done((f32[128,128]{1,0:T(8,128)S(1)}, f32[128,128]{1,0:T(8,128)S(1)}, u32[]{:S(2)}, u32[]{:S(2)}) %collective-permute-start.28) | collective-permute-done | bytes 65568 | tf_op jit(solution)/shard_map/ppermute | solution.py:380
  96.8 0.8 shard_map.121
  97.6 3.5 %all-to-all-start.1 = ((f32[8,128,128]{2,1,0:T(8,128)}), f32[8,128,128]{2,1,0:T(8,128)S(1)}, u32[]{:S(2)}, u32[]{:S(2)}) async-start(f32[8,128,128]{2,1,0:T(8,128)} %bitcast.5), calls=%async_computation.1 | async-start | bytes 1048576 | tf_op jit(solution)/shard_map/all_to_all | solution.py:390
  101.2 1.9 %collective-permute-start.24 = (f32[2,512,128]{2,1,0:T(8,128)}, f32[2,512,128]{2,1,0:T(8,128)}, u32[]{:S(2)}, u32[]{:S(2)}) collective-permute-start(f32[2,512,128]{2,1,0:T(8,128)} %copy-done.2), channel_id=1, source_target_pairs={{0,4},{1,2},{2,1},{3,7},{4,0},{5,6},{6,5},{7,3},{8,12},{9,10},{10,... | collective-permute-start | bytes 1572872 | tf_op jit(solution)/shard_map/ppermute | solution.py:80
  103.0 5.8 %all-to-all-done.1 = f32[8,128,128]{2,1,0:T(8,128)S(1)} async-done(((f32[8,128,128]{2,1,0:T(8,128)}), f32[8,128,128]{2,1,0:T(8,128)S(1)}, u32[]{:S(2)}, u32[]{:S(2)}) %all-to-all-start.1) | async-done | bytes 524320 | tf_op jit(solution)/shard_map/all_to_all | solution.py:390
  108.8 4.5 %collective-permute-done.24.x_odd = f32[2,512,128]{2,1,0:T(8,128)} collective-permute-done((f32[2,512,128]{2,1,0:T(8,128)}, f32[2,512,128]{2,1,0:T(8,128)}, u32[]{:S(2)}, u32[]{:S(2)}) %collective-permute-start.24) | collective-permute-done | bytes 524320 | tf_op jit(solution)/shard_map/ppermute | solution.py:80
  113.3 1.6 %copy-done.1 = f32[2,4,512,128]{3,2,1,0:T(8,128)S(1)} copy-done((f32[2,4,512,128]{3,2,1,0:T(8,128)S(1)}, f32[2,4,512,128]{3,2,1,0:T(8,128)}, u32[]{:S(2)}) %copy-start.1) | copy-done | bytes 2097176
  114.9 1.2 shard_map.117
  116.1 1.4 %collective-permute-start.25 = (f32[2,2,128,128]{3,2,1,0:T(8,128)S(1)}, f32[2,2,128,128]{3,2,1,0:T(8,128)S(1)}, u32[]{:S(2)}, u32[]{:S(2)}) collective-permute-start(f32[2,2,128,128]{3,2,1,0:T(8,128)S(1)} %get-tuple-element.78), channel_id=1, source_target_pairs={{0,4},{1,5},{2,6},{3,7},{4,0},{5,1},{6,2},{7,3},{8,12},{9,13},{10,... | collective-permute-start | bytes 786440 | tf_op jit(solution)/shard_map/ppermute | solution.py:80
  117.5 0.7 collective-permute-start.26
  118.2 10.8 %collective-permute-done.25.y_even = f32[2,2,128,128]{3,2,1,0:T(8,128)S(1)} collective-permute-done((f32[2,2,128,128]{3,2,1,0:T(8,128)S(1)}, f32[2,2,128,128]{3,2,1,0:T(8,128)S(1)}, u32[]{:S(2)}, u32[]{:S(2)}) %collective-permute-start.25) | collective-permute-done | bytes 262176 | tf_op jit(solution)/shard_map/ppermute | solution.py:80
  128.9 0.9 shard_map.118
  129.8 1.0 shard_map.122
  (44 shorter events, 1.1 us)
Async XLA Ops:
  1.8 12.5 %collective-permute-start = (f32[2,128,128]{2,1,0:T(8,128)S(1)}, f32[2,128,128]{2,1,0:T(8,128)S(1)}, u32[]{:S(2)}, u32[]{:S(2)}) collective-permute-start(f32[2,128,128]{2,1,0:T(8,128)S(1)} %get-tuple-element.49), channel_id=1, source_target_pairs={{0,4},{1,5},{2,6},{3,7},{4,0},{5,1},{6,2},{7,3},{8,12},{9,13},{10,... | collective-permute-start | bytes 393224 | tf_op jit(solution)/shard_map/ppermute | solution.py:80
  4.8 11.5 %collective-permute-start.1 = (f32[2,128,128]{2,1,0:T(8,128)S(1)}, f32[2,128,128]{2,1,0:T(8,128)S(1)}, u32[]{:S(2)}, u32[]{:S(2)}) collective-permute-start(f32[2,128,128]{2,1,0:T(8,128)S(1)} %get-tuple-element.50), channel_id=1, source_target_pairs={{0,2},{1,3},{2,0},{3,1},{4,8},{5,9},{6,10},{7,11},{8,4},{9,5},{10,... | collective-permute-start | bytes 393224 | tf_op jit(solution)/shard_map/ppermute | solution.py:80
  6.3 10.1 %collective-permute-start.2 = (f32[2,128,128]{2,1,0:T(8,128)S(1)}, f32[2,128,128]{2,1,0:T(8,128)S(1)}, u32[]{:S(2)}, u32[]{:S(2)}) collective-permute-start(f32[2,128,128]{2,1,0:T(8,128)S(1)} %get-tuple-element.51), channel_id=1, source_target_pairs={{0,4},{1,5},{2,6},{3,7},{4,0},{5,1},{6,2},{7,3},{8,12},{9,13},{10,... | collective-permute-start | bytes 393224 | tf_op jit(solution)/shard_map/ppermute | solution.py:80
  7.9 8.6 %collective-permute-start.3 = (f32[2,128,128]{2,1,0:T(8,128)S(1)}, f32[2,128,128]{2,1,0:T(8,128)S(1)}, u32[]{:S(2)}, u32[]{:S(2)}) collective-permute-start(f32[2,128,128]{2,1,0:T(8,128)S(1)} %get-tuple-element.52), channel_id=1, source_target_pairs={{0,2},{1,3},{2,0},{3,1},{4,8},{5,9},{6,10},{7,11},{8,4},{9,5},{10,... | collective-permute-start | bytes 393224 | tf_op jit(solution)/shard_map/ppermute | solution.py:80
  10.7 10.8 %collective-permute-start.4 = (f32[2,256,128]{2,1,0:T(8,128)S(1)}, f32[2,256,128]{2,1,0:T(8,128)S(1)}, u32[]{:S(2)}, u32[]{:S(2)}) collective-permute-start(f32[2,256,128]{2,1,0:T(8,128)S(1)} %get-tuple-element.53), channel_id=1, source_target_pairs={{0,1},{1,0},{2,3},{3,2},{4,5},{5,4},{6,7},{7,6},{8,9},{9,8},{10,11... | collective-permute-start | bytes 786440 | tf_op jit(solution)/shard_map/ppermute | solution.py:80
  14.3 7.2 %collective-permute-start.5 = (f32[2,256,128]{2,1,0:T(8,128)S(1)}, f32[2,256,128]{2,1,0:T(8,128)S(1)}, u32[]{:S(2)}, u32[]{:S(2)}) collective-permute-start(f32[2,256,128]{2,1,0:T(8,128)S(1)} %get-tuple-element.54), channel_id=1, source_target_pairs={{0,8},{1,2},{2,1},{3,11},{4,12},{5,6},{6,5},{7,15},{8,0},{9,10},{1... | collective-permute-start | bytes 786440 | tf_op jit(solution)/shard_map/ppermute | solution.py:80
  16.4 5.2 %collective-permute-start.6 = (f32[2,2,128,128]{3,2,1,0:T(8,128)S(1)}, f32[2,2,128,128]{3,2,1,0:T(8,128)S(1)}, u32[]{:S(2)}, u32[]{:S(2)}) collective-permute-start(f32[2,2,128,128]{3,2,1,0:T(8,128)S(1)} %shard_map.105), channel_id=1, source_target_pairs={{0,1},{1,0},{2,3},{3,2},{4,5},{5,4},{6,7},{7,6},{8,9},{9,8},{10,11... | collective-permute-start | bytes 786440 | tf_op jit(solution)/shard_map/ppermute | solution.py:80
  16.5 7.0 %collective-permute-start.7 = (f32[2,2,128,128]{3,2,1,0:T(8,128)S(1)}, f32[2,2,128,128]{3,2,1,0:T(8,128)S(1)}, u32[]{:S(2)}, u32[]{:S(2)}) collective-permute-start(f32[2,2,128,128]{3,2,1,0:T(8,128)S(1)} %shard_map.106), channel_id=1, source_target_pairs={{0,8},{1,2},{2,1},{3,11},{4,12},{5,6},{6,5},{7,15},{8,0},{9,10},{1... | collective-permute-start | bytes 786440 | tf_op jit(solution)/shard_map/ppermute | solution.py:80
  30.7 12.7 %collective-permute-start.8 = (f32[2,512,128]{2,1,0:T(8,128)S(1)}, f32[2,512,128]{2,1,0:T(8,128)S(1)}, u32[]{:S(2)}, u32[]{:S(2)}) collective-permute-start(f32[2,512,128]{2,1,0:T(8,128)S(1)} %get-tuple-element.61), channel_id=1, source_target_pairs={{0,1},{1,0},{2,3},{3,2},{4,5},{5,4},{6,7},{7,6},{8,9},{9,8},{10,11... | collective-permute-start | bytes 1572872 | tf_op jit(solution)/shard_map/ppermute | solution.py:80
  30.7 6.5 %collective-permute-start.13 = (f32[512,128]{1,0:T(8,128)S(1)}, f32[512,128]{1,0:T(8,128)S(1)}, u32[]{:S(2)}, u32[]{:S(2)}) collective-permute-start(f32[512,128]{1,0:T(8,128)S(1)} %get-tuple-element.67), channel_id=1, source_target_pairs={{0,8},{1,2},{2,1},{3,11},{4,12},{5,6},{6,5},{7,15},{8,0},{9,10},{1... | collective-permute-start | bytes 786440 | tf_op jit(solution)/shard_map/ppermute | solution.py:80
  32.9 7.2 %collective-permute-start.16 = (f32[512,128]{1,0:T(8,128)S(1)}, f32[512,128]{1,0:T(8,128)S(1)}, u32[]{:S(2)}, u32[]{:S(2)}) collective-permute-start(f32[512,128]{1,0:T(8,128)S(1)} %get-tuple-element.70), channel_id=1, source_target_pairs={{0,8},{1,2},{2,1},{3,11},{4,12},{5,6},{6,5},{7,15},{8,0},{9,10},{1... | collective-permute-start | bytes 786440 | tf_op jit(solution)/shard_map/ppermute | solution.py:80
  37.3 12.1 %collective-permute-start.14 = (f32[256,128]{1,0:T(8,128)S(1)}, f32[256,128]{1,0:T(8,128)S(1)}, u32[]{:S(2)}, u32[]{:S(2)}) collective-permute-start(f32[256,128]{1,0:T(8,128)S(1)} %get-tuple-element.68.sent_even), channel_id=1, source_target_pairs={{0,4},{1,5},{2,6},{3,7},{4,0},{5,1},{6,2},{7,3},{8,12},{9,13},{10,... | collective-permute-start | bytes 393224 | tf_op jit(solution)/shard_map/ppermute | solution.py:80
  39.8 9.8 %collective-permute-start.15 = (f32[256,128]{1,0:T(8,128)S(1)}, f32[256,128]{1,0:T(8,128)S(1)}, u32[]{:S(2)}, u32[]{:S(2)}) collective-permute-start(f32[256,128]{1,0:T(8,128)S(1)} %get-tuple-element.69.sent_odd), channel_id=1, source_target_pairs={{0,2},{1,3},{2,0},{3,1},{4,8},{5,9},{6,10},{7,11},{8,4},{9,5},{10,... | collective-permute-start | bytes 393224 | tf_op jit(solution)/shard_map/ppermute | solution.py:80
  40.1 13.3 %collective-permute-start.17 = (f32[256,128]{1,0:T(8,128)S(1)}, f32[256,128]{1,0:T(8,128)S(1)}, u32[]{:S(2)}, u32[]{:S(2)}) collective-permute-start(f32[256,128]{1,0:T(8,128)S(1)} %get-tuple-element.71.sent_even), channel_id=1, source_target_pairs={{0,4},{1,5},{2,6},{3,7},{4,0},{5,1},{6,2},{7,3},{8,12},{9,13},{10,... | collective-permute-start | bytes 393224 | tf_op jit(solution)/shard_map/ppermute | solution.py:80
  43.0 10.7 %collective-permute-start.18 = (f32[256,128]{1,0:T(8,128)S(1)}, f32[256,128]{1,0:T(8,128)S(1)}, u32[]{:S(2)}, u32[]{:S(2)}) collective-permute-start(f32[256,128]{1,0:T(8,128)S(1)} %get-tuple-element.72.sent_odd), channel_id=1, source_target_pairs={{0,2},{1,3},{2,0},{3,1},{4,8},{5,9},{6,10},{7,11},{8,4},{9,5},{10,... | collective-permute-start | bytes 393224 | tf_op jit(solution)/shard_map/ppermute | solution.py:80
  43.4 17.1 %collective-permute-start.9 = (f32[256,128]{1,0:T(8,128)S(1)}, f32[256,128]{1,0:T(8,128)S(1)}, u32[]{:S(2)}, u32[]{:S(2)}) collective-permute-start(f32[256,128]{1,0:T(8,128)S(1)} %get-tuple-element.62.sent_even), channel_id=1, source_target_pairs={{0,4},{1,5},{2,6},{3,7},{4,0},{5,1},{6,2},{7,3},{8,12},{9,13},{10,... | collective-permute-start | bytes 393224 | tf_op jit(solution)/shard_map/ppermute | solution.py:80
  49.3 13.1 %collective-permute-start.10 = (f32[256,128]{1,0:T(8,128)S(1)}, f32[256,128]{1,0:T(8,128)S(1)}, u32[]{:S(2)}, u32[]{:S(2)}) collective-permute-start(f32[256,128]{1,0:T(8,128)S(1)} %get-tuple-element.63.sent_odd), channel_id=1, source_target_pairs={{0,2},{1,3},{2,0},{3,1},{4,8},{5,9},{6,10},{7,11},{8,4},{9,5},{10,... | collective-permute-start | bytes 393224 | tf_op jit(solution)/shard_map/ppermute | solution.py:80
  49.6 13.0 %collective-permute-start.11 = (f32[256,128]{1,0:T(8,128)S(1)}, f32[256,128]{1,0:T(8,128)S(1)}, u32[]{:S(2)}, u32[]{:S(2)}) collective-permute-start(f32[256,128]{1,0:T(8,128)S(1)} %get-tuple-element.65.sent_even), channel_id=1, source_target_pairs={{0,4},{1,5},{2,6},{3,7},{4,0},{5,1},{6,2},{7,3},{8,12},{9,13},{10,... | collective-permute-start | bytes 393224 | tf_op jit(solution)/shard_map/ppermute | solution.py:80
  53.4 9.2 %collective-permute-start.12 = (f32[256,128]{1,0:T(8,128)S(1)}, f32[256,128]{1,0:T(8,128)S(1)}, u32[]{:S(2)}, u32[]{:S(2)}) collective-permute-start(f32[256,128]{1,0:T(8,128)S(1)} %get-tuple-element.66.sent_odd), channel_id=1, source_target_pairs={{0,2},{1,3},{2,0},{3,1},{4,8},{5,9},{6,10},{7,11},{8,4},{9,5},{10,... | collective-permute-start | bytes 393224 | tf_op jit(solution)/shard_map/ppermute | solution.py:80
  53.7 9.6 %collective-permute-start.21 = (f32[512,128]{1,0:T(8,128)S(1)}, f32[512,128]{1,0:T(8,128)S(1)}, u32[]{:S(2)}, u32[]{:S(2)}) collective-permute-start(f32[512,128]{1,0:T(8,128)S(1)} %shard_map.113.far_re), channel_id=1, source_target_pairs={{0,8},{1,2},{2,1},{3,11},{4,12},{5,6},{6,5},{7,15},{8,0},{9,10},{1... | collective-permute-start | bytes 786440 | tf_op jit(solution)/shard_map/ppermute | solution.py:80
  60.6 6.4 %collective-permute-start.22 = (f32[512,128]{1,0:T(8,128)S(1)}, f32[512,128]{1,0:T(8,128)S(1)}, u32[]{:S(2)}, u32[]{:S(2)}) collective-permute-start(f32[512,128]{1,0:T(8,128)S(1)} %shard_map.115.far_im), channel_id=1, source_target_pairs={{0,8},{1,2},{2,1},{3,11},{4,12},{5,6},{6,5},{7,15},{8,0},{9,10},{1... | collective-permute-start | bytes 786440 | tf_op jit(solution)/shard_map/ppermute | solution.py:80
  62.5 4.5 %collective-permute-start.19 = (f32[512,128]{1,0:T(8,128)S(1)}, f32[512,128]{1,0:T(8,128)S(1)}, u32[]{:S(2)}, u32[]{:S(2)}) collective-permute-start(f32[512,128]{1,0:T(8,128)S(1)} %shard_map.109.near_re), channel_id=1, source_target_pairs={{0,1},{1,0},{2,3},{3,2},{4,5},{5,4},{6,7},{7,6},{8,9},{9,8},{10,11... | collective-permute-start | bytes 786440 | tf_op jit(solution)/shard_map/ppermute | solution.py:80
  62.7 4.3 %collective-permute-start.20 = (f32[512,128]{1,0:T(8,128)S(1)}, f32[512,128]{1,0:T(8,128)S(1)}, u32[]{:S(2)}, u32[]{:S(2)}) collective-permute-start(f32[512,128]{1,0:T(8,128)S(1)} %shard_map.111.near_im), channel_id=1, source_target_pairs={{0,1},{1,0},{2,3},{3,2},{4,5},{5,4},{6,7},{7,6},{8,9},{9,8},{10,11... | collective-permute-start | bytes 786440 | tf_op jit(solution)/shard_map/ppermute | solution.py:80
  74.4 16.4 %copy-start = (f32[2,4,512,128]{3,2,1,0:T(8,128)}, f32[2,4,512,128]{3,2,1,0:T(8,128)S(1)}, u32[]{:S(2)}) copy-start(f32[2,4,512,128]{3,2,1,0:T(8,128)S(1)} %get-tuple-element.74.accum) | copy-start | bytes 6291460
  74.4 23.2 %copy-start.2 = (f32[2,512,128]{2,1,0:T(8,128)}, f32[2,512,128]{2,1,0:T(8,128)S(1)}, u32[]{:S(2)}) copy-start(f32[2,512,128]{2,1,0:T(8,128)S(1)} %get-tuple-element.76) | copy-start | bytes 1572868
  74.4 23.2 %copy-start.3 = (f32[2,512,128]{2,1,0:T(8,128)}, f32[2,512,128]{2,1,0:T(8,128)S(1)}, u32[]{:S(2)}) copy-start(f32[2,512,128]{2,1,0:T(8,128)S(1)} %get-tuple-element.75) | copy-start | bytes 1572868
  74.4 2.0 %collective-permute-start.27 = (f32[1024,128]{1,0:T(8,128)S(1)}, f32[1024,128]{1,0:T(8,128)S(1)}, u32[]{:S(2)}, u32[]{:S(2)}) collective-permute-start(f32[1024,128]{1,0:T(8,128)S(1)} %bitcast.15), channel_id=1, source_target_pairs={{0,1},{1,0},{2,3},{3,2},{4,5},{5,4},{6,7},{7,6},{8,9},{9,8},{10,11... | collective-permute-start | bytes 1572872 | tf_op jit(solution)/shard_map/ppermute | solution.py:380
  90.8 5.9 %collective-permute-start.28 = (f32[128,128]{1,0:T(8,128)S(1)}, f32[128,128]{1,0:T(8,128)S(1)}, u32[]{:S(2)}, u32[]{:S(2)}) collective-permute-start(f32[128,128]{1,0:T(8,128)S(1)} %shard_map.120.left), channel_id=1, source_target_pairs={{0,16},{1,17},{2,18},{3,19},{4,20},{5,21},{6,22},{7,23},{8,24},{9,... | collective-permute-start | bytes 196616 | tf_op jit(solution)/shard_map/ppermute | solution.py:380
  97.6 11.2 %all-to-all-start.1 = ((f32[8,128,128]{2,1,0:T(8,128)}), f32[8,128,128]{2,1,0:T(8,128)S(1)}, u32[]{:S(2)}, u32[]{:S(2)}) async-start(f32[8,128,128]{2,1,0:T(8,128)} %bitcast.5), calls=%async_computation.1 | async-start | bytes 1048576 | tf_op jit(solution)/shard_map/all_to_all | solution.py:390
  101.1 7.7 %collective-permute-start.23 = (f32[2,512,128]{2,1,0:T(8,128)}, f32[2,512,128]{2,1,0:T(8,128)S(1)}, u32[]{:S(2)}, u32[]{:S(2)}) collective-permute-start(f32[2,512,128]{2,1,0:T(8,128)} %copy-done.3), channel_id=1, source_target_pairs={{0,1},{1,0},{2,3},{3,2},{4,5},{5,4},{6,7},{7,6},{8,9},{9,8},{10,11... | collective-permute-start | bytes 1572872 | tf_op jit(solution)/shard_map/ppermute | solution.py:80
  101.2 12.1 %collective-permute-start.24 = (f32[2,512,128]{2,1,0:T(8,128)}, f32[2,512,128]{2,1,0:T(8,128)}, u32[]{:S(2)}, u32[]{:S(2)}) collective-permute-start(f32[2,512,128]{2,1,0:T(8,128)} %copy-done.2), channel_id=1, source_target_pairs={{0,4},{1,2},{2,1},{3,7},{4,0},{5,6},{6,5},{7,3},{8,12},{9,10},{10,... | collective-permute-start | bytes 1572872 | tf_op jit(solution)/shard_map/ppermute | solution.py:80
  108.8 21.0 %collective-permute-start.29 = (f32[1024,128]{1,0:T(8,128)S(1)}, f32[1024,128]{1,0:T(8,128)S(1)}, u32[]{:S(2)}, u32[]{:S(2)}) collective-permute-start(f32[1024,128]{1,0:T(8,128)S(1)} %bitcast.11), channel_id=1, source_target_pairs={{0,1},{1,0},{2,3},{3,2},{4,5},{5,4},{6,7},{7,6},{8,9},{9,8},{10,11... | collective-permute-start | bytes 1572872 | tf_op jit(solution)/shard_map/ppermute | solution.py:380
  113.3 1.6 %copy-start.1 = (f32[2,4,512,128]{3,2,1,0:T(8,128)S(1)}, f32[2,4,512,128]{3,2,1,0:T(8,128)}, u32[]{:S(2)}) copy-start(f32[2,4,512,128]{3,2,1,0:T(8,128)} %copy-done) | copy-start | bytes 6291460
  116.1 12.9 %collective-permute-start.25 = (f32[2,2,128,128]{3,2,1,0:T(8,128)S(1)}, f32[2,2,128,128]{3,2,1,0:T(8,128)S(1)}, u32[]{:S(2)}, u32[]{:S(2)}) collective-permute-start(f32[2,2,128,128]{3,2,1,0:T(8,128)S(1)} %get-tuple-element.78), channel_id=1, source_target_pairs={{0,4},{1,5},{2,6},{3,7},{4,0},{5,1},{6,2},{7,3},{8,12},{9,13},{10,... | collective-permute-start | bytes 786440 | tf_op jit(solution)/shard_map/ppermute | solution.py:80
  117.5 11.5 %collective-permute-start.26 = (f32[2,2,128,128]{3,2,1,0:T(8,128)S(1)}, f32[2,2,128,128]{3,2,1,0:T(8,128)S(1)}, u32[]{:S(2)}, u32[]{:S(2)}) collective-permute-start(f32[2,2,128,128]{3,2,1,0:T(8,128)S(1)} %get-tuple-element.79), channel_id=1, source_target_pairs={{0,2},{1,3},{2,0},{3,1},{4,8},{5,9},{6,10},{7,11},{8,4},{9,5},{10,... | collective-permute-start | bytes 786440 | tf_op jit(solution)/shard_map/ppermute | solution.py:80
